TPU v7x, 32 devices: a whole 2x2x4 slice. The times are simulated.
32 devices in a mesh: expert: 8 (over z, x), dp: 4 (over y, core).
Axes of the slice: x: 2, y: 2, z: 4, core: 2. Of those that a mesh axis runs over, the one named last changes fastest.
Arguments:
- features: bfloat16 [4096, 32, 64], P(('expert', 'dp')), may hold values from -1 to 1
- spacing: float32 [4096, 32], P(('expert', 'dp')), may hold values from 0.02 to 0.3
- targets: float32 [3, 4096], P(None, ('expert', 'dp')), may hold values from 0 to 1
- ray_length: int32 [4096], P(('expert', 'dp')), may hold values from 1 to 32, as said below
- cell_id: int32 [4096, 32], P(('expert', 'dp')), may hold values from 0 to 15, as said below
- slot_rank: int32 [4096, 32], P(('expert', 'dp')), may hold values from -1 to 383, as said below
- image_id: int32 [4096], P(('expert', 'dp')), may hold values from 0 to 511, as said below
- params: float32 [16, 848, 256], P('expert'), may hold values from -5 to 5
- first_moment: float32 [16, 848, 256], P('expert'), may hold values from -0.75 to 0.75
- second_moment: float32 [16, 848, 256], P('expert'), may hold values from 1e-06 to 0.01
- code_table: float32 [512, 64], P(('expert', 'dp')), may hold values from -6 to 6
- table_first: float32 [512, 64], P(('expert', 'dp')), may hold values from -0.75 to 0.75
- table_second: float32 [512, 64], P(('expert', 'dp')), may hold values from 1e-06 to 0.01
Outputs:
- ray_loss: float32 [4096], P(('expert', 'dp'))
- new_params: float32 [16, 848, 256], P('expert')
- new_first_moment: float32 [16, 848, 256], P('expert')
- new_second_moment: float32 [16, 848, 256], P('expert')
- new_code_table: float32 [512, 64], P(('expert', 'dp'))
- new_table_first: float32 [512, 64], P(('expert', 'dp'))
- new_table_second: float32 [512, 64], P(('expert', 'dp'))
Inputs may be any that keep to these rules, and one draw needn't show every extreme that they name: `ray_length`: rays form aligned blocks of 128, one a device, in the order of the axes expert then dp. In every block the lengths sum to 3072 and some ray has all 32 samples. `cell_id`: also given for samples at or beyond their ray's length, where it is unused. `slot_rank`: for a sample below its ray's length: its rank among the live samples of its block of 128 rays that have the same cell_id, counted ray by ray and along each ray; -1 for the other samples. No block has more than 384 live samples of one cell_id; in every block some cell_id has exactly 384, and one cell_id has 384 in every block. `image_id`: A ray of block b names an image from b * 16 to (b + 1) * 16 - 1.
All inputs are finite; a program needn't handle non-finite values.
Results may differ from a plain program's by a relative error of at most 0.0046.
Values may be sent and summed in bfloat16 or wider, within the bound.
A program may use at most 128 MiB of HBM per device.

v0:
```python
import jax
import jax.numpy as jnp
from jax import lax
from jax.sharding import PartitionSpec as P

NET_WIDTH = 256
CODE_WIDTH = 64
ENC_WIDTH = 64
LAYERS = 4
SAMPLES = 32


BETA_ONE = 0.9
BETA_TWO = 0.999
LEARN_RATE = 0.001
ADAM_EPS = 1e-08
CORRECT_ONE = 1.0 - 0.9**10
CORRECT_TWO = 1.0 - 0.999**10


def adam_update(param_now, gradient, moment_one, moment_two):
    new_one = BETA_ONE * moment_one + (1.0 - BETA_ONE) * gradient
    new_two = BETA_TWO * moment_two + (1.0 - BETA_TWO) * gradient * gradient
    update = LEARN_RATE * (new_one / CORRECT_ONE) / (jnp.sqrt(new_two / CORRECT_TWO) + ADAM_EPS)
    return (param_now - update, new_one, new_two)


def composite(raw_out, spacing, live_mask, targets):
    density = jax.nn.softplus(raw_out[0])
    colors = jax.nn.sigmoid(raw_out[1:4])
    optical = density * spacing * live_mask
    before = jnp.cumsum(optical, axis=1) - optical
    weight = jnp.exp(-before) * (1.0 - jnp.exp(-optical))
    render = jnp.sum(weight[None] * colors, axis=2)
    return 0.5 * jnp.sum((render - targets) ** 2, axis=0)


def place_rows(rows, slot_index, slots_all):
    blank = jnp.zeros((slots_all,) + rows.shape[1:], rows.dtype)
    return blank.at[slot_index].set(rows, mode="drop")


def pick_rows(buffer, slot_index):
    return jnp.take(buffer, slot_index, axis=0, mode="fill", fill_value=0)


def hidden_pass(weights_bf, inputs):
    head_row = ENC_WIDTH + (LAYERS - 1) * NET_WIDTH
    activations = [inputs]
    preacts = []
    current = inputs
    row_start = 0
    row_count = ENC_WIDTH
    for layer_index in range(LAYERS):
        matrix = weights_bf[:, row_start : row_start + row_count, :]
        bias_row = weights_bf[:, head_row + 9 + layer_index, :].astype(jnp.float32)
        preact = (
            jnp.einsum("enr,erw->enw", current, matrix, preferred_element_type=jnp.float32)
            + bias_row[:, None, :]
        )
        current = jnp.maximum(preact, 0.0).astype(jnp.bfloat16)
        preacts.append(preact)
        activations.append(current)
        row_start = row_start + row_count
        row_count = NET_WIDTH
    return (activations, preacts)


def hidden_grads(weights_bf, activations, preacts, upstream):
    weight_grads = [None] * LAYERS
    bias_grads = [None] * LAYERS
    for layer_index in reversed(range(LAYERS)):
        pre_grad = jnp.where(preacts[layer_index] > 0, upstream, 0.0).astype(jnp.bfloat16)
        weight_grads[layer_index] = jnp.einsum(
            "enr,enw->erw", activations[layer_index], pre_grad, preferred_element_type=jnp.float32
        )
        bias_grads[layer_index] = jnp.sum(pre_grad, axis=1, dtype=jnp.float32)
        if layer_index > 0:
            row_start = ENC_WIDTH + (layer_index - 1) * NET_WIDTH
            upstream = jnp.einsum(
                "enw,erw->enr",
                pre_grad,
                weights_bf[:, row_start : row_start + NET_WIDTH, :],
                preferred_element_type=jnp.float32,
            )
    return (weight_grads, bias_grads)


def assemble(weight_grads, bias_grads, hidden_grad, code_grad_head, bias_grad_head):
    held_count = hidden_grad.shape[0]
    pieces = list(weight_grads) + [
        hidden_grad,
        jnp.pad(code_grad_head, ((0, 0), (0, 0), (0, NET_WIDTH - CODE_WIDTH))),
        jnp.pad(bias_grad_head, ((0, 0), (0, NET_WIDTH - 4)))[:, None, :],
        jnp.stack(bias_grads, axis=1),
        jnp.zeros((held_count, 7 - LAYERS, NET_WIDTH), jnp.float32),
    ]
    return jnp.concatenate(pieces, axis=1)


def shards(
    features,
    spacing,
    targets,
    ray_length,
    cell_id,
    slot_rank,
    image_id,
    params,
    first_moment,
    second_moment,
    code_table,
    table_first,
    table_second,
):
    ray_rows = features.shape[0]
    sample_count = ray_rows * SAMPLES
    groups = lax.axis_size("expert")
    held_count = params.shape[0]
    experts_all = held_count * groups
    capacity = 2 * (sample_count * 3 // 4 // experts_all)
    slots_all = experts_all * capacity
    head_row = ENC_WIDTH + (LAYERS - 1) * NET_WIDTH
    weights_bf = params.astype(jnp.bfloat16)
    table_rows = code_table.shape[0]
    block_index = lax.axis_index("expert") * lax.axis_size("dp") + lax.axis_index("dp")
    local_image = image_id - block_index * table_rows
    picker = (local_image[:, None] == jnp.arange(table_rows, dtype=jnp.int32)[None, :]).astype(
        jnp.bfloat16
    )
    ray_code = jnp.dot(
        picker, code_table.astype(jnp.bfloat16), preferred_element_type=jnp.float32
    ).astype(jnp.bfloat16)
    position = jnp.arange(SAMPLES, dtype=jnp.int32)
    live_mask = (position[None, :] < ray_length[:, None]).astype(jnp.float32)
    flat_rank = slot_rank.reshape(sample_count)
    slot_index = jnp.where(
        flat_rank >= 0, cell_id.reshape(sample_count) * capacity + flat_rank, slots_all
    )
    positions = features.reshape(sample_count, ENC_WIDTH)
    sample_code = jnp.broadcast_to(ray_code[:, None, :], (ray_rows, SAMPLES, CODE_WIDTH)).reshape(
        sample_count, CODE_WIDTH
    )
    outgoing = place_rows(
        jnp.concatenate([positions, sample_code], axis=1), slot_index, slots_all
    ).reshape(experts_all, capacity, ENC_WIDTH + CODE_WIDTH)
    arrived = lax.all_to_all(outgoing, "expert", split_axis=0, concat_axis=1, tiled=True)
    hidden_head = weights_bf[:, head_row : head_row + 4, :]
    inputs = arrived[:, :, :ENC_WIDTH]
    code_rows = arrived[:, :, ENC_WIDTH:]
    activations, preacts = hidden_pass(weights_bf, inputs)
    raw_out = jnp.einsum(
        "enw,ecw->enc", activations[-1], hidden_head, preferred_element_type=jnp.float32
    )
    code_head = weights_bf[:, head_row + 4 : head_row + 8, :CODE_WIDTH]
    raw_out = raw_out + jnp.einsum(
        "enk,eck->enc", code_rows, code_head, preferred_element_type=jnp.float32
    )
    raw_out = raw_out + weights_bf[:, head_row + 8, :4].astype(jnp.float32)[:, None, :]
    returned = lax.all_to_all(raw_out, "expert", split_axis=1, concat_axis=0, tiled=True)
    raw_samples = pick_rows(returned.reshape(slots_all, 4), slot_index)
    raw_grid = raw_samples.T.reshape(4, ray_rows, SAMPLES)

    def loss_of(raw_in):
        return composite(raw_in, spacing, live_mask, targets)

    ray_loss, pullback = jax.vjp(loss_of, raw_grid)
    (raw_grad,) = pullback(jnp.ones_like(ray_loss))
    cotangent = raw_grad.reshape(4, sample_count).T.astype(jnp.bfloat16)
    cot_slots = place_rows(cotangent, slot_index, slots_all).reshape(experts_all, capacity, 4)
    cot_in = lax.all_to_all(cot_slots, "expert", split_axis=0, concat_axis=1, tiled=True)
    upstream = jnp.einsum("enc,ecw->enw", cot_in, hidden_head, preferred_element_type=jnp.float32)
    weight_grads, bias_grads = hidden_grads(weights_bf, activations, preacts, upstream)
    hidden_grad = jnp.einsum(
        "enc,enw->ecw", cot_in, activations[-1], preferred_element_type=jnp.float32
    )
    code_grad_head = jnp.einsum(
        "enc,enk->eck", cot_in, code_rows, preferred_element_type=jnp.float32
    )
    bias_grad_head = jnp.sum(cot_in, axis=1, dtype=jnp.float32)
    code_back = jnp.einsum("enc,eck->enk", cot_in, code_head, preferred_element_type=jnp.float32)
    code_back = code_back.reshape(held_count, groups * capacity // 2, 2 * CODE_WIDTH)
    code_slot_grad = lax.all_to_all(
        code_back, "expert", split_axis=1, concat_axis=0, tiled=True
    ).reshape(slots_all, CODE_WIDTH)
    local_grad = assemble(weight_grads, bias_grads, hidden_grad, code_grad_head, bias_grad_head)
    param_grad = lax.psum(local_grad, "dp")
    sample_code_grad = pick_rows(code_slot_grad, slot_index).reshape(ray_rows, SAMPLES, CODE_WIDTH)
    ray_code_grad = jnp.sum(sample_code_grad, axis=1)
    table_grad = lax.dot_general(
        picker.astype(jnp.float32),
        ray_code_grad,
        (((0,), (0,)), ((), ())),
        precision=lax.Precision.HIGHEST,
        preferred_element_type=jnp.float32,
    )
    new_params, new_first, new_second = adam_update(params, param_grad, first_moment, second_moment)
    new_table, new_table_first, new_table_second = adam_update(
        code_table, table_grad, table_first, table_second
    )
    return (
        ray_loss,
        new_params,
        new_first,
        new_second,
        new_table,
        new_table_first,
        new_table_second,
    )


def solution(mesh):
    return jax.shard_map(
        shards,
        mesh=mesh,
        in_specs=(
            P(("expert", "dp"), None, None),
            P(("expert", "dp"), None),
            P(None, ("expert", "dp")),
            P(("expert", "dp")),
            P(("expert", "dp"), None),
            P(("expert", "dp"), None),
            P(("expert", "dp")),
            P("expert", None, None),
            P("expert", None, None),
            P("expert", None, None),
            P(("expert", "dp"), None),
            P(("expert", "dp"), None),
            P(("expert", "dp"), None),
        ),
        out_specs=(
            P(("expert", "dp")),
            P("expert", None, None),
            P("expert", None, None),
            P("expert", None, None),
            P(("expert", "dp"), None),
            P(("expert", "dp"), None),
            P(("expert", "dp"), None),
        ),
        check_vma=False,
    )
```

profile of v0, /device:TPU:0, one launch (start us, length us, event | category | flops | bytes accessed | tf_op | source)
XLA Modules:
  0.0 286.6 jit_solution(14919669906394410517)
XLA Ops:
  9.9 2.5 copy.93
  13.4 13.5 %scatter_custom_fusion = bf16[6144,128]{1,0:T(8,128)(2,1)} fusion(s32[4096]{0:T(1024)S(1)} %bitcast.80, bf16[4096,64]{1,0:T(8,128)(2,1)} %bitcast.72, bf16[]{:T(256)} %constant.118, bf16[4096,64]{1,0:T(8,128)(2,1)S(1)} %bitcast.71, bf16[]{:T(256)} %constant.35.clone.1), kind=kCustom, calls=%fused_computation.37 | custom fusion | flops 2097152 | bytes 3145732 | tf_op jit(solution)/shard_map/scatter | solution.py:40
  26.9 7.8 %all-to-all-start = ((bf16[16,384,128]{2,1,0:T(8,128)(2,1)}), bf16[16,384,128]{2,1,0:T(8,128)(2,1)S(1)}, u32[]{:S(2)}, u32[]{:S(2)}) async-start(bf16[16,384,128]{2,1,0:T(8,128)(2,1)} %bitcast.68), calls=%async_computation | async-start | bytes 3145728 | tf_op jit(solution)/shard_map/all_to_all | solution.py:147
  35.9 35.9 %all-to-all-done = bf16[16,384,128]{2,1,0:T(8,128)(2,1)S(1)} async-done(((bf16[16,384,128]{2,1,0:T(8,128)(2,1)}), bf16[16,384,128]{2,1,0:T(8,128)(2,1)S(1)}, u32[]{:S(2)}, u32[]{:S(2)}) %all-to-all-start) | async-done | bytes 1572896 | tf_op jit(solution)/shard_map/all_to_all | solution.py:147
  73.7 4.1 %fusion.2 = (u8[3072,256]{1,0:T(8,128)(4,1)}, f32[2,3072,256]{2,1,0:T(8,128)S(1)}) fusion(f32[2,256]{1,0:T(2,128)S(1)} %bitcast.86, bf16[2,848,256]{2,1,0:T(8,128)(2,1)} %copy-done.9, bf16[2,3072,128]{1,2,0:T(8,128)(2,1)S(1)} %all_to_all.51), kind=kOutput, calls=%fused_computation.32 | convolution fusion | flops 209977344 | bytes 7931904 | tf_op jit(solution)/shard_map/enr,erw->enw/dot_general | solution.py:58
  77.8 3.1 %fusion.3 = (u8[3072,256]{1,0:T(8,128)(4,1)}, f32[2,3072,256]{2,1,0:T(8,128)S(1)}) fusion(f32[2,256]{1,0:T(2,128)S(1)} %get-tuple-element.38, bf16[2,848,256]{2,1,0:T(8,128)(2,1)S(1)} %copy-done.10, f32[2,3072,256]{2,1,0:T(8,128)S(1)} %get-tuple-element.28, f32[2,256]{1,0:T(2,128)S(1)} %bitcast.87), kind=kOutput, calls=%fused_computation.33 | convolution fusion | flops 818675712 | bytes 13635584 | tf_op jit(solution)/shard_map/enr,erw->enw/dot_general | solution.py:58
  80.9 3.1 %fusion.4 = (u8[3072,256]{1,0:T(8,128)(4,1)}, f32[2,3072,256]{2,1,0:T(8,128)S(1)}) fusion(f32[2,256]{1,0:T(2,128)S(1)} %get-tuple-element.37, bf16[2,848,256]{2,1,0:T(8,128)(2,1)S(1)} %copy-done.10, f32[2,3072,256]{2,1,0:T(8,128)S(1)} %get-tuple-element.26, f32[2,256]{1,0:T(2,128)S(1)} %get-tuple-element.38), kind=kOutput, calls=%fused_computation.34 | convolution fusion | flops 818675712 | bytes 13635584 | tf_op jit(solution)/shard_map/enr,erw->enw/dot_general | solution.py:58
  84.0 3.1 %fusion.5 = (u8[3072,256]{1,0:T(8,128)(4,1)}, f32[2,3072,256]{2,1,0:T(8,128)S(1)}) fusion(f32[2,256]{1,0:T(2,128)S(1)} %bitcast.83, bf16[2,848,256]{2,1,0:T(8,128)(2,1)S(1)} %copy-done.10, f32[2,3072,256]{2,1,0:T(8,128)S(1)} %get-tuple-element.24, f32[2,256]{1,0:T(2,128)S(1)} %get-tuple-element.37), kind=kOutput, calls=%fused_computation.35 | convolution fusion | flops 818675712 | bytes 13635584 | tf_op jit(solution)/shard_map/enr,erw->enw/dot_general | solution.py:58
  89.9 2.9 %copy.96 = f32[2,3072,4]{2,0,1:T(2,128)S(1)} copy(f32[2,3072,4]{1,2,0:T(4,128)S(1)} %fusion) | data formatting | bytes 196608 | tf_op jit(solution)/shard_map/add | solution.py:159
  92.8 5.6 %reshape.184 = f32[8,1,3072]{2,1,0:T(1,128)} reshape(f32[3072,2,4]{2,1,0:T(2,128)S(1)} %bitcast.65) | data formatting | bytes 196608
  98.5 3.9 %all-to-all-start.1 = ((f32[8,1,3072]{2,1,0:T(1,128)}), f32[8,1,3072]{2,1,0:T(1,128)S(1)}, u32[]{:S(2)}, u32[]{:S(2)}) async-start(f32[8,1,3072]{2,1,0:T(1,128)} %reshape.184), calls=%async_computation.1 | async-start | bytes 196608 | tf_op jit(solution)/shard_map/all_to_all | solution.py:160
  102.3 7.1 %all-to-all-done.1 = f32[8,1,3072]{2,1,0:T(1,128)S(1)} async-done(((f32[8,1,3072]{2,1,0:T(1,128)}), f32[8,1,3072]{2,1,0:T(1,128)S(1)}, u32[]{:S(2)}, u32[]{:S(2)}) %all-to-all-start.1) | async-done | bytes 98336 | tf_op jit(solution)/shard_map/all_to_all | solution.py:160
  110.8 6.6 %reshape.185 = f32[3072,2,4]{2,1,0:T(2,128)} reshape(f32[8,3072]{1,0:T(8,128)S(1)} %reduce.14) | data formatting | bytes 196608
  117.4 2.2 copy.97
  119.6 14.1 %gather_fusion = f32[4096,4]{1,0:T(8,128)} fusion(f32[6144,4]{1,0:T(8,128)S(1)} %bitcast.60, s32[4096]{0:T(1024)S(1)} %broadcast_clamp_fusion), kind=kCustom, calls=%fused_computation | custom fusion | bytes 147456 | tf_op jit(solution)/shard_map/jit(_take)/gather | solution.py:44
  133.7 2.2 copy.98
  138.1 11.4 %scatter_custom_fusion.1 = bf16[6144,4]{1,0:T(8,128)(2,1)S(1)} fusion(s32[4096]{0:T(1024)S(1)} %bitcast.82, bf16[4096,4]{1,0:T(8,128)(2,1)S(1)} %copy.113, bf16[]{:T(256)} %constant.35.clone.1), kind=kCustom, calls=%fused_computation.49 | custom fusion | bytes 49154 | tf_op jit(solution)/shard_map/scatter | solution.py:40
  150.3 9.4 %all_to_all.66 = bf16[16,384,4]{1,2,0:T(4,128)(2,1)S(1)} all-to-all(bf16[16,384,4]{1,2,0:T(4,128)(2,1)S(1)} %copy.114), channel_id=1, replica_groups=mesh['expert'=8,'dp'=4] {'expert'}, dimensions={0} | all-to-all | bytes 98304 | tf_op jit(solution)/shard_map/all_to_all | solution.py:171
  159.7 3.6 %fusion.16 = f32[2,4,256]{2,1,0:T(4,128)S(1)} fusion(bf16[2,3072,4]{1,2,0:T(4,128)(2,1)S(1)} %bitcast.73, f32[2,3072,256]{2,1,0:T(8,128)} %copy-done.3, f32[2,256]{1,0:T(2,128)S(1)} %bitcast.85), kind=kOutput, calls=%fused_computation.47 | convolution fusion | flops 17301504 | bytes 6350848 | tf_op jit(solution)/shard_map/enc,enw->ecw/dot_general | solution.py:174
  166.7 2.3 fusion.14
  172.1 3.0 %convert_reduce_fusion.3 = (f32[2,256]{1,0:T(2,128)S(1)}, bf16[2,3072,256]{2,1,0:T(8,128)(2,1)}) fusion(bf16[2,3072,256]{2,1,0:T(8,128)(2,1)S(1)} %get-tuple-element.32, bf16[2,848,256]{2,1,0:T(8,128)(2,1)S(1)} %copy-done.11, u8[3072,256]{1,0:T(8,128)(4,1)S(1)} %copy-done.16), kind=kOutput, calls=%fused_computation.16 | convolution fusion | flops 817888768 | bytes 7342080 | tf_op jit(solution)/shard_map/enw,erw->enr/dot_general | solution.py:80
  176.6 7.0 %copy.121 = f32[2,1536,128]{2,0,1:T(2,128)} copy(f32[2,1536,128]{2,1,0:T(8,128)} %reshape.134) | data formatting | bytes 3145728 | tf_op jit(solution)/shard_map/reshape | solution.py:182
  183.6 3.6 %all-to-all-start.3 = ((f32[2,1536,128]{2,0,1:T(2,128)}), f32[2,1536,128]{2,0,1:T(2,128)S(1)}, u32[]{:S(2)}, u32[]{:S(2)}) async-start(f32[2,1536,128]{2,0,1:T(2,128)} %copy.121), calls=%async_computation.3 | async-start | bytes 3145728 | tf_op jit(solution)/shard_map/all_to_all | solution.py:183
  187.6 2.7 fusion.24
  190.4 5.4 %fusion.12 = f32[2,256,256]{2,1,0:T(8,128)} fusion(bf16[2,3072,256]{2,1,0:T(8,128)(2,1)S(1)} %copy-done.13, f32[2,3072,256]{2,1,0:T(8,128)} %copy-done.1, f32[2,256]{1,0:T(2,128)S(1)} %get-tuple-element.38), kind=kOutput, calls=%fused_computation.43 | convolution fusion | flops 810024960 | bytes 9963520 | tf_op jit(solution)/shard_map/enr,enw->erw/dot_general | solution.py:74
  195.8 2.3 fusion.10
  198.1 7.2 %concatenate.7 = f32[2,848,256]{2,1,0:T(8,128)} concatenate(f32[2,64,256]{2,1,0:T(8,128)S(1)} %fusion.24, f32[2,256,256]{2,1,0:T(8,128)} %fusion.10, f32[2,256,256]{2,1,0:T(8,128)} %fusion.12, f32[2,256,256]{2,1,0:T(8,128)} %fusion.14, f32[2,4,256]{2,1,0:T(4,128)S(1)} %fusion.16, f32[2,4,256]{2,1,0:T(4,128)S(1)} %pad.16, f32[2,1,256]{2,1,0:T(1,128)S(1)} %broadcast_in_dim.84, ...), dimensions={1} | concatenate | bytes 3473408 | tf_op jit(solution)/shard_map/concatenate | solution.py:98
  205.9 46.4 %all-reduce.6.cloned.1.call-done = f32[2,848,256]{2,1,0:T(8,128)} async-done(((f32[2,848,256]{2,1,0:T(8,128)}), f32[2,848,256]{2,1,0:T(8,128)}) %all-reduce.6.cloned.1.call-update) | async-done | bytes 1736720 | tf_op jit(solution)/shard_map/psum | solution.py:187
  252.3 5.5 %divide_subtract_fusion = (f32[2,848,256]{2,1,0:T(8,128)}, f32[2,848,256]{2,1,0:T(8,128)}, f32[2,848,256]{2,1,0:T(8,128)}) fusion(f32[2,848,256]{2,1,0:T(8,128)S(1)} %copy-done.5, f32[2,848,256]{2,1,0:T(8,128)} %all-reduce.6.cloned.1.call-done, f32[2,848,256]{2,1,0:T(8,128)} %param.21, f32[2,848,256]{2,1,0:T(8,128)} %param.22), kind=kLoop, calls=%fused_computation.30 | loop fusion | flops 5210112 | bytes 12156928 | tf_op jit(solution)/shard_map/sub | solution.py:25
  259.1 2.4 reshape.135
  261.6 14.1 %gather_fusion.1 = f32[4096,64]{1,0:T(8,128)} fusion(f32[6144,64]{1,0:T(8,128)S(1)} %reshape.135, s32[4096]{0:T(1024)S(1)} %broadcast_clamp_fusion), kind=kCustom, calls=%fused_computation.1 | custom fusion | bytes 2113536 | tf_op jit(solution)/shard_map/jit(_take)/gather | solution.py:44
  275.7 2.8 select_reduce_fusion
  (135 shorter events, 25.1 us)
Async XLA Ops:
  13.4 21.4 %copy-start.4 = (f32[2,848,256]{2,1,0:T(8,128)S(1)}, f32[2,848,256]{2,1,0:T(8,128)}, u32[]{:S(2)}) copy-start(f32[2,848,256]{2,1,0:T(8,128)} %param.20) | copy-start | bytes 5210116
  26.9 44.8 %all-to-all-start = ((bf16[16,384,128]{2,1,0:T(8,128)(2,1)}), bf16[16,384,128]{2,1,0:T(8,128)(2,1)S(1)}, u32[]{:S(2)}, u32[]{:S(2)}) async-start(bf16[16,384,128]{2,1,0:T(8,128)(2,1)} %bitcast.68), calls=%async_computation | async-start | bytes 3145728 | tf_op jit(solution)/shard_map/all_to_all | solution.py:147
  73.7 16.1 %copy-start.6 = (bf16[2,3072,128]{1,2,0:T(8,128)(2,1)}, bf16[2,3072,128]{1,2,0:T(8,128)(2,1)S(1)}, u32[]{:S(2)}) copy-start(bf16[2,3072,128]{1,2,0:T(8,128)(2,1)S(1)} %all_to_all.51) | copy-start | bytes 4718596
  73.7 4.1 %copy-start.10 = (bf16[2,848,256]{2,1,0:T(8,128)(2,1)S(1)}, bf16[2,848,256]{2,1,0:T(8,128)(2,1)}, u32[]{:S(2)}) copy-start(bf16[2,848,256]{2,1,0:T(8,128)(2,1)} %copy-done.9) | copy-start | bytes 2605060
  77.8 3.1 %copy-start = (f32[2,3072,256]{2,1,0:T(8,128)}, f32[2,3072,256]{2,1,0:T(8,128)S(1)}, u32[]{:S(2)}) copy-start(f32[2,3072,256]{2,1,0:T(8,128)S(1)} %get-tuple-element.28) | copy-start | bytes 18874372
  80.8 3.1 %copy-start.1 = (f32[2,3072,256]{2,1,0:T(8,128)}, f32[2,3072,256]{2,1,0:T(8,128)S(1)}, u32[]{:S(2)}) copy-start(f32[2,3072,256]{2,1,0:T(8,128)S(1)} %get-tuple-element.26) | copy-start | bytes 18874372
  84.0 3.1 %copy-start.2 = (f32[2,3072,256]{2,1,0:T(8,128)}, f32[2,3072,256]{2,1,0:T(8,128)S(1)}, u32[]{:S(2)}) copy-start(f32[2,3072,256]{2,1,0:T(8,128)S(1)} %get-tuple-element.24) | copy-start | bytes 18874372
  87.1 2.6 copy-start.3
  98.5 10.9 %all-to-all-start.1 = ((f32[8,1,3072]{2,1,0:T(1,128)}), f32[8,1,3072]{2,1,0:T(1,128)S(1)}, u32[]{:S(2)}, u32[]{:S(2)}) async-start(f32[8,1,3072]{2,1,0:T(1,128)} %reshape.184), calls=%async_computation.1 | async-start | bytes 196608 | tf_op jit(solution)/shard_map/all_to_all | solution.py:160
  119.6 16.6 %copy-start.20 = (f32[128,32]{0,1:T(8,128)S(1)}, f32[128,32]{0,1:T(8,128)}, u32[]{:S(2)}) copy-start(f32[128,32]{0,1:T(8,128)} %param.14) | copy-start | bytes 49156
  119.6 16.6 %copy-start.24 = (s32[128]{0:T(128)S(1)}, s32[128]{0:T(128)}, u32[]{:S(2)}) copy-start(s32[128]{0:T(128)} %param.16) | copy-start | bytes 1540
  133.7 2.9 %copy-start.25 = (f32[3,128]{1,0:T(4,128)S(1)}, f32[3,128]{1,0:T(4,128)}, u32[]{:S(2)}) copy-start(f32[3,128]{1,0:T(4,128)} %param.15) | copy-start | bytes 4612
  159.7 3.6 %copy-start.7 = (bf16[2,3072,128]{1,2,0:T(8,128)(2,1)S(1)}, bf16[2,3072,128]{1,2,0:T(8,128)(2,1)}, u32[]{:S(2)}) copy-start(bf16[2,3072,128]{1,2,0:T(8,128)(2,1)} %copy-done.6) | copy-start | bytes 4718596
  159.7 3.9 %copy-start.11 = (bf16[2,848,256]{2,1,0:T(8,128)(2,1)S(1)}, bf16[2,848,256]{2,1,0:T(8,128)(2,1)}, u32[]{:S(2)}) copy-start(bf16[2,848,256]{2,1,0:T(8,128)(2,1)} %copy-done.9) | copy-start | bytes 2605060
  163.6 2.4 slice-start.2
  164.5 2.2 slice-start.3
  166.7 2.4 copy-start.18
  169.0 1.4 copy-start.17
  170.4 1.7 copy-start.12
  170.4 1.7 copy-start.16
  172.1 3.1 %copy-start.14 = (bf16[2,3072,256]{2,1,0:T(8,128)(2,1)}, bf16[2,3072,256]{2,1,0:T(8,128)(2,1)S(1)}, u32[]{:S(2)}) copy-start(bf16[2,3072,256]{2,1,0:T(8,128)(2,1)S(1)} %get-tuple-element.32) | copy-start | bytes 9437188
  176.6 10.9 %copy-start.8 = (bf16[2,3072,128]{1,2,0:T(8,128)(2,1)S(1)}, bf16[2,3072,128]{1,2,0:T(8,128)(2,1)}, u32[]{:S(2)}) copy-start(bf16[2,3072,128]{1,2,0:T(8,128)(2,1)} %copy-done.6) | copy-start | bytes 4718596
  183.6 74.1 %all-to-all-start.3 = ((f32[2,1536,128]{2,0,1:T(2,128)}), f32[2,1536,128]{2,0,1:T(2,128)S(1)}, u32[]{:S(2)}, u32[]{:S(2)}) async-start(f32[2,1536,128]{2,0,1:T(2,128)} %copy.121), calls=%async_computation.3 | async-start | bytes 3145728 | tf_op jit(solution)/shard_map/all_to_all | solution.py:183
  187.2 65.1 %all-reduce.6.cloned.1.call-start = ((), (), s32[]{:S(2)}) async-start(), calls=%async_computation.4 | async-start | bytes 3473408 | tf_op jit(solution)/shard_map/psum | solution.py:187
  187.5 2.8 copy-start.13
  187.6 8.2 %slice-start = ((s8[6291456]{0:T(1024)(128)(4,1)}), s8[4194304]{0:T(1024)(128)(4,1)S(1)}, s32[]{:S(2)}) async-start(s8[6291456]{0:T(1024)(128)(4,1)} %bitcast.61), calls=%async_computation.5 | async-start | bytes 8388608
  190.4 5.4 %slice-start.1 = ((s8[6291456]{0:T(1024)(128)(4,1)}), s8[2097152]{0:T(1024)(128)(4,1)S(1)}, s32[]{:S(2)}) async-start(s8[6291456]{0:T(1024)(128)(4,1)} %bitcast.61), calls=%async_computation.6 | async-start | bytes 4194304
  190.4 5.4 %copy-start.15 = (bf16[2,3072,256]{2,1,0:T(8,128)(2,1)S(1)}, bf16[2,3072,256]{2,1,0:T(8,128)(2,1)}, u32[]{:S(2)}) copy-start(bf16[2,3072,256]{2,1,0:T(8,128)(2,1)} %copy-done.14) | copy-start | bytes 9437188
  198.1 54.2 %copy-start.5 = (f32[2,848,256]{2,1,0:T(8,128)S(1)}, f32[2,848,256]{2,1,0:T(8,128)}, u32[]{:S(2)}) copy-start(f32[2,848,256]{2,1,0:T(8,128)} %param.20) | copy-start | bytes 5210116
  261.6 17.0 %copy-start.21 = (f32[16,64]{1,0:T(8,128)S(1)}, f32[16,64]{1,0:T(8,128)}, u32[]{:S(2)}) copy-start(f32[16,64]{1,0:T(8,128)} %param.23) | copy-start | bytes 12292
  261.6 17.0 %copy-start.22 = (f32[16,64]{1,0:T(8,128)S(1)}, f32[16,64]{1,0:T(8,128)}, u32[]{:S(2)}) copy-start(f32[16,64]{1,0:T(8,128)} %param.24) | copy-start | bytes 12292
  261.6 16.9 %copy-start.23 = (f32[16,64]{1,0:T(8,128)S(1)}, f32[16,64]{1,0:T(8,128)}, u32[]{:S(2)}) copy-start(f32[16,64]{1,0:T(8,128)} %param.25) | copy-start | bytes 12292
  (2 other events, 2.1 us)
Sparse Core Ops, SparseCore 0:
  205.4 46.8 all-reduce.5
where the time goes:
time: 291 us; the launch traced here: 287 us
  local copies, waits for them, and re-layouts  91.2 us (31%)
  waiting for transfers between devices  89.3 us (31%)
  matrix products  40.9 us (14%)
  other arithmetic  25.4 us (9%)
  starting transfers between devices  15.6 us (5%)
  between operations  14.9 us (5%)
  blocking collectives  9.38 us (3%)
    psum x1, waiting for transfers between devices, shards(): param_grad = lax.psum(local_grad, 'dp')  46.4 us
    all_to_all x1, waiting for transfers between devices, shards(): lax.all_to_all(outgoing, 'expert', split_axis=0, concat_axis=1, tiled=True)  35.9 us
    gather x3, local copies, waits for them, and re-layouts, pick_rows(): return jnp.take(buffer, slot_index, axis=0, mode='fill', fill_value=0)  30.4 us
    unnamed x66, local copies, waits for them, and re-layouts  18.5 us
    scatter x1, other arithmetic, place_rows(): return blank.at[slot_index].set(rows, mode='drop')  13.5 us
    dot_general x4, matrix products, hidden_pass(): jnp.einsum('enr,erw->enw', current, matrix, preferred_element_type=jnp.fl...  13.4 us
    dot_general x4, matrix products, hidden_grads(): jnp.einsum('enr,enw->erw', activations[layer_index], pre_grad, preferred_...  12.7 us
    scatter x1, local copies, waits for them, and re-layouts, place_rows(): return blank.at[slot_index].set(rows, mode='drop')  11.4 us
  transfers between devices with their start and end apart: 4, of which 3 were waited for; matrix products, arithmetic and copies ran while one was open for 8% of the time, Pallas kernels for 0%

commit v1 on v0

v1 whole, which is shorter than its diff:
```python
import functools

import jax
import jax.numpy as jnp
from jax import lax
from jax.experimental import pallas as pl
from jax.experimental.pallas import tpu as pltpu
from jax.sharding import PartitionSpec as P

NET_WIDTH = 256
CODE_WIDTH = 64
ENC_WIDTH = 64
LAYERS = 4
SAMPLES = 32
HEAD_ROW = ENC_WIDTH + (LAYERS - 1) * NET_WIDTH
LANES = 128

BETA_ONE = 0.9
BETA_TWO = 0.999
LEARN_RATE = 0.001
ADAM_EPS = 1e-08
CORRECT_ONE = 1.0 - 0.9**10
CORRECT_TWO = 1.0 - 0.999**10

MESH = pl.DeviceIdType.MESH
VMEM = pl.BlockSpec(memory_space=pltpu.VMEM)
SMEM = pl.BlockSpec(memory_space=pltpu.SMEM)
F32 = jnp.float32
BF16 = jnp.bfloat16
NN = (((1,), (0,)), ((), ()))
NT = (((1,), (1,)), ((), ()))
TN = (((0,), (0,)), ((), ()))


def dot(left, right, dims=NN, precision=None):
    return lax.dot_general(left, right, dims, precision=precision, preferred_element_type=F32)


def exact(left, right, dims=NN):
    return dot(left, right, dims, lax.Precision.HIGHEST)


def adam_update(param_now, gradient, moment_one, moment_two):
    new_one = BETA_ONE * moment_one + (1.0 - BETA_ONE) * gradient
    new_two = BETA_TWO * moment_two + (1.0 - BETA_TWO) * gradient * gradient
    update = LEARN_RATE * (new_one / CORRECT_ONE) / (jnp.sqrt(new_two / CORRECT_TWO) + ADAM_EPS)
    return (param_now - update, new_one, new_two)


def lane_block(index):
    return pl.ds(pl.multiple_of(index * LANES, LANES), LANES)


def move_rows(count, move):
    step = 32

    def body(block, carry):
        for inner in range(step):
            move(block * step + inner)
        return carry

    lax.fori_loop(0, count // step, body, 0)


def place_kernel(groups, cap, cap_up, slot_ref, feat_ref, out_ref, rows, table):
    table[...] = jnp.zeros_like(table)

    def turn(i, carry):
        block = feat_ref[i].astype(F32)
        rows[lane_block(i), :] = jnp.concatenate([block, block], axis=0).T
        return carry

    lax.fori_loop(0, SAMPLES, turn, 0)

    def move(s):
        table[pl.ds(slot_ref[s], 1), :] = rows[pl.ds(s, 1), :]

    move_rows(rows.shape[0], move)
    low = lax.broadcasted_iota(jnp.int32, (cap, LANES), 1) < ENC_WIDTH

    def pack(g, carry):
        first = table[pl.ds(pl.multiple_of(2 * g * cap_up, LANES), cap), :]
        second = table[pl.ds(pl.multiple_of((2 * g + 1) * cap_up, LANES), cap), :]
        out_ref[g] = jnp.where(low, first, second).astype(BF16)
        return carry

    lax.fori_loop(0, groups, pack, 0)


def greet(groups, me):
    barrier = pltpu.get_barrier_semaphore()

    def body(k, carry):
        pl.semaphore_signal(
            barrier, 1, device_id={"expert": lax.rem(me + k, groups)}, device_id_type=MESH
        )
        return carry

    lax.fori_loop(1, groups, body, 0)
    return barrier


def pad_first(wt_ref, m0):
    m0[...] = jnp.zeros_like(m0)
    for h in range(2):
        m0[h, ENC_WIDTH * h : ENC_WIDTH * (h + 1), :] = wt_ref[h, 0:ENC_WIDTH, :]


def layer_matrix(wt_ref, m0, h, layer):
    if layer == 0:
        return m0[h]
    start = ENC_WIDTH + (layer - 1) * NET_WIDTH
    return wt_ref[h, start : start + NET_WIDTH, :]


def tail_rows(wt_ref, h):
    return wt_ref[h, HEAD_ROW : HEAD_ROW + 16, :]


def forward(wt_ref, m0, h, current, keep=None):
    tail = tail_rows(wt_ref, h).astype(F32)
    for layer in range(LAYERS):
        preact = dot(current, layer_matrix(wt_ref, m0, h, layer))
        preact = preact + tail[9 + layer : 10 + layer, :]
        current = jnp.maximum(preact, 0.0).astype(BF16)
        if keep is not None:
            keep(layer, current)
    return current


def forward_kernel(
    groups, cap, cap_up, disp, wt, tail_msg, arr, raw_out, recv, msg, back, m0, s1, r1, s2, r2
):
    me = lax.axis_index("expert")
    barrier = greet(groups, me)
    pl.semaphore_wait(barrier, groups - 1)

    def out_copy(k):
        peer = lax.rem(me + k, groups)
        return pltpu.make_async_remote_copy(
            disp.at[peer], recv.at[k], s1.at[k], r1.at[k],
            device_id={"expert": peer}, device_id_type=MESH,
        )

    def back_copy(k):
        peer = lax.rem(me + groups - k, groups)
        return pltpu.make_async_remote_copy(
            msg.at[k], back.at[me], s2.at[k], r2.at[k],
            device_id={"expert": peer}, device_id_type=MESH,
        )

    def start(k, carry):
        out_copy(k).start()
        return carry

    lax.fori_loop(1, groups, start, 0)
    pad_first(wt, m0)

    def process(k, block):
        arr[k] = block
        msg[k, :, cap_up:] = tail_msg[...]
        if cap_up > cap:
            msg[k, :, cap:cap_up] = jnp.zeros((8, cap_up - cap), F32)
        for h in range(2):
            act = forward(wt, m0, h, block)
            raw = dot(tail_rows(wt, h), act, NT)
            msg[k, 4 * h : 4 * h + 4, 0:cap] = raw[0:4]

    process(0, disp[me])
    back[me] = msg[0]

    def step(k, carry):
        out_copy(k).wait_recv()
        process(k, recv[k])
        back_copy(k).start()
        return carry

    lax.fori_loop(1, groups, step, 0)

    def finish(k, carry):
        out_copy(k).wait_send()
        back_copy(k).wait_send()
        back_copy(k).wait_recv()
        return carry

    lax.fori_loop(1, groups, finish, 0)
    raw_out[...] = back[...]


def home_kernel(
    groups, cap_up, slot_ref, raw_ref, cell_ref, spacing_ref, length_ref, target_ref, image_ref,
    code_ref, first_ref, second_ref, loss_out, msg_out, code_out, first_out, second_out,
    rows, table, eight, mix, queries, shift,
):
    tiles = cap_up // LANES
    filler = jnp.zeros((LANES - 8, LANES), F32)

    def widen(g, carry):
        for t in range(tiles):
            piece = raw_ref[g, :, t * LANES : (t + 1) * LANES]
            turned = jnp.concatenate([piece, filler], axis=0).T
            for h in range(2):
                start = pl.multiple_of((2 * g + h) * cap_up + t * LANES, LANES)
                table[pl.ds(start, LANES), :] = turned
        block = pl.ds(pl.multiple_of(8 * g, 8), 8)
        queries[block, :] = raw_ref[g, :, cap_up : cap_up + CODE_WIDTH]
        shift[block, :] = jnp.broadcast_to(
            raw_ref[g, :, cap_up + CODE_WIDTH : cap_up + CODE_WIDTH + 1], (8, LANES)
        )
        return carry

    lax.fori_loop(0, groups, widen, 0)
    table[pl.ds(2 * groups * cap_up, 8), :] = jnp.zeros((8, LANES), F32)

    def take(s):
        rows[pl.ds(s, 1), :] = table[pl.ds(slot_ref[s], 1), :]

    move_rows(rows.shape[0], take)

    def narrow(i, carry):
        eight[pl.ds(pl.multiple_of(8 * i, 8), 8), :] = rows[lane_block(i), :].T[0:8]
        return carry

    lax.fori_loop(0, SAMPLES, narrow, 0)
    table[...] = jnp.zeros_like(table)

    table_rows = code_ref.shape[0]
    pick = (
        lax.broadcasted_iota(jnp.int32, (table_rows, LANES), 0) == image_ref[...]
    ).astype(F32)
    code_bf = code_ref[...].astype(BF16).astype(F32)
    ray_code = exact(code_bf, pick, TN)
    mix[...] = exact(queries[...], ray_code) + shift[...]

    cell = cell_ref[...]
    odd = lax.rem(cell, 2) == 1
    row = lax.broadcasted_iota(jnp.int32, (SAMPLES, LANES), 0)
    live = row < length_ref[...]
    raws = tuple(
        jnp.where(
            odd, eight[pl.ds(4 + c, SAMPLES, 8), :], eight[pl.ds(c, SAMPLES, 8), :]
        )
        for c in range(4)
    )

    def add_code(g, raws):
        part = mix[pl.ds(pl.multiple_of(8 * g, 8), 8), :]
        raws = list(raws)
        for h in range(2):
            hit = cell == 2 * g + h
            for c in range(4):
                j = 4 * h + c
                raws[c] = raws[c] + jnp.where(hit, part[j : j + 1, :], 0.0)
        return tuple(raws)

    raws = lax.fori_loop(0, groups, add_code, raws)
    raws = [jnp.where(live, raw, 0.0) for raw in raws]
    spacing = spacing_ref[...]
    density = jnp.maximum(raws[0], 0.0) + jnp.log1p(jnp.exp(-jnp.abs(raws[0])))
    colors = [jax.nn.sigmoid(raw) for raw in raws[1:]]
    tau = jnp.where(live, density * spacing, 0.0)
    square_row = lax.broadcasted_iota(jnp.int32, (SAMPLES, SAMPLES), 0)
    square_col = lax.broadcasted_iota(jnp.int32, (SAMPLES, SAMPLES), 1)
    before = exact((square_col < square_row).astype(F32), tau)
    through = jnp.exp(-before)
    fade = jnp.exp(-tau)
    weight = through * (1.0 - fade)
    gaps = [
        jnp.sum(weight * colors[c], axis=0, keepdims=True) - target_ref[c : c + 1, :]
        for c in range(3)
    ]
    loss_out[...] = 0.5 * (gaps[0] * gaps[0] + gaps[1] * gaps[1] + gaps[2] * gaps[2])
    pull = gaps[0] * colors[0] + gaps[1] * colors[1] + gaps[2] * colors[2]
    after = exact((square_col > square_row).astype(F32), pull * weight)
    tau_grad = pull * through * fade - after
    grads = [tau_grad * spacing * jax.nn.sigmoid(raws[0])]
    for c in range(3):
        grads.append(gaps[c] * weight * colors[c] * (1.0 - colors[c]))
    cots = [jnp.where(live, grad, 0.0).astype(BF16).astype(F32) for grad in grads]
    for c in range(4):
        eight[pl.ds(c, SAMPLES, 8), :] = jnp.where(odd, 0.0, cots[c])
        eight[pl.ds(4 + c, SAMPLES, 8), :] = jnp.where(odd, cots[c], 0.0)

    def gather_code(g, carry):
        pieces = []
        for h in range(2):
            hit = cell == 2 * g + h
            for c in range(4):
                pieces.append(jnp.sum(jnp.where(hit, cots[c], 0.0), axis=0, keepdims=True))
        mix[pl.ds(pl.multiple_of(8 * g, 8), 8), :] = jnp.concatenate(pieces, axis=0)
        return carry

    lax.fori_loop(0, groups, gather_code, 0)
    totals = mix[...]
    query_grad = exact(totals, ray_code, NT)
    table_grad = exact(exact(totals, pick, NT), queries[...], TN)
    new_code, new_first, new_second = adam_update(
        code_ref[...], table_grad, first_ref[...], second_ref[...]
    )
    code_out[...] = new_code
    first_out[...] = new_first
    second_out[...] = new_second
    queries[...] = query_grad

    def widen_back(i, carry):
        piece = eight[pl.ds(pl.multiple_of(8 * i, 8), 8), :]
        rows[lane_block(i), :] = jnp.concatenate([piece, filler], axis=0).T
        return carry

    lax.fori_loop(0, SAMPLES, widen_back, 0)

    def put(s):
        table[pl.ds(slot_ref[s], 1), :] = rows[pl.ds(s, 1), :]

    move_rows(rows.shape[0], put)

    def pack(g, carry):
        for t in range(tiles):
            start = [pl.multiple_of((2 * g + h) * cap_up + t * LANES, LANES) for h in range(2)]
            both = table[pl.ds(start[0], LANES), :] + table[pl.ds(start[1], LANES), :]
            msg_out[g, :, t * LANES : (t + 1) * LANES] = both.T[0:8]
        part = queries[pl.ds(pl.multiple_of(8 * g, 8), 8), :]
        msg_out[g, :, cap_up:] = jnp.concatenate(
            [part, jnp.zeros((8, LANES - CODE_WIDTH), F32)], axis=1
        )
        return carry

    lax.fori_loop(0, groups, pack, 0)


def backward_kernel(
    groups, cap, cap_up, msg, wt, arr, grad_out, recv, act, pre, m0, head, code_sum, cot_sum,
    grad, half_in, sum_out, sum_in, full, s1, r1, s2, r2,
):
    me = lax.axis_index("expert")
    my_dp = lax.axis_index("dp")
    core = lax.rem(my_dp, 2)
    near = my_dp + 1 - 2 * core
    far = my_dp + 2 - 4 * lax.rem(my_dp // 2, 2)
    barrier = greet(groups, me)
    for peer in (near, far):
        pl.semaphore_signal(barrier, 1, device_id={"dp": peer}, device_id_type=MESH)
    pl.semaphore_wait(barrier, groups + 1)

    def out_copy(k):
        peer = lax.rem(me + k, groups)
        return pltpu.make_async_remote_copy(
            msg.at[peer], recv.at[k], s1.at[k], r1.at[k],
            device_id={"expert": peer}, device_id_type=MESH,
        )

    def start(k, carry):
        out_copy(k).start()
        return carry

    lax.fori_loop(1, groups, start, 0)
    pad_first(wt, m0)
    head[...] = jnp.zeros_like(head)
    for h in range(2):
        head[h, 4 * h : 4 * h + 4, :] = tail_rows(wt, h).astype(F32)[0:4]

    def again(k, carry):
        block = pl.ds(pl.multiple_of(k * cap, 16), cap)
        for h in range(2):

            def keep(layer, value):
                act[layer, h, block, :] = value

            forward(wt, m0, h, arr[block, :], keep)
        return carry

    lax.fori_loop(0, groups, again, 0)
    recv[0] = msg[me]

    def arrive(k, carry):
        out_copy(k).wait()
        return carry

    lax.fori_loop(1, groups, arrive, 0)

    chunks = []
    for layer in range(LAYERS):
        first = 0 if layer == 0 else ENC_WIDTH + (layer - 1) * NET_WIDTH
        last = HEAD_ROW + 16 if layer == LAYERS - 1 else ENC_WIDTH + layer * NET_WIDTH
        chunks.append(pl.ds(first, last - first))

    def near_copy(layer):
        return pltpu.make_async_remote_copy(
            grad.at[1 - core, chunks[layer]], half_in.at[chunks[layer]],
            s2.at[0, layer], r2.at[0, layer], device_id={"dp": near}, device_id_type=MESH,
        )

    def far_copy(layer):
        return pltpu.make_async_remote_copy(
            sum_out.at[chunks[layer]], sum_in.at[chunks[layer]],
            s2.at[1, layer], r2.at[1, layer], device_id={"dp": far}, device_id_type=MESH,
        )

    def full_copy(layer):
        return pltpu.make_async_remote_copy(
            full.at[core, chunks[layer]], full.at[core, chunks[layer]],
            s2.at[2, layer], r2.at[2, layer], device_id={"dp": near}, device_id_type=MESH,
        )

    def second_stage(layer):
        near_copy(layer).wait_recv()
        rows = chunks[layer]
        sum_out[rows, :] = (grad[core, rows, :] + half_in[rows, :]).astype(BF16)
        far_copy(layer).start()

    def third_stage(layer):
        far_copy(layer).wait_recv()
        rows = chunks[layer]
        full[core, rows, :] = sum_out[rows, :].astype(F32) + sum_in[rows, :].astype(F32)
        full_copy(layer).start()

    bias = [[None] * LAYERS for _ in range(2)]
    top = LAYERS - 1
    hidden = []

    for h in range(2):

        def back(k, carry):
            block = pl.ds(pl.multiple_of(k * cap, 16), cap)
            cot = recv[k, :, 0:cap].astype(BF16)
            up = dot(cot, head[h].astype(BF16), TN)
            sums = []
            for layer in reversed(range(LAYERS)):
                value = jnp.where(act[layer, h, block, :].astype(F32) > 0, up, 0.0).astype(BF16)
                pre[layer, h, block, :] = value
                sums.append(
                    carry[top - layer] + jnp.sum(value.astype(F32), axis=0, keepdims=True)
                )
                if layer > 0:
                    up = dot(value, layer_matrix(wt, m0, h, layer), NT)
            heads = carry[LAYERS] + dot(cot, act[top, h, block, :])
            return tuple(sums) + (heads,)

        zero = jnp.zeros((1, NET_WIDTH), F32)
        done = lax.fori_loop(
            0, groups, back, (zero,) * LAYERS + (jnp.zeros((8, NET_WIDTH), F32),)
        )
        for layer in range(LAYERS):
            bias[h][layer] = done[top - layer]
        hidden.append(done[LAYERS])

    code_sum[...] = jnp.zeros_like(code_sum)
    cot_sum[...] = jnp.zeros_like(cot_sum)

    def add_codes(k, carry):
        code_sum[...] += recv[k, :, cap_up:]
        cot_sum[...] += jnp.broadcast_to(
            jnp.sum(recv[k, :, 0:cap], axis=1, keepdims=True), (8, LANES)
        )
        return carry

    lax.fori_loop(0, groups, add_codes, 0)
    codes = jnp.concatenate([code_sum[...], jnp.zeros((8, NET_WIDTH - LANES), F32)], axis=1)
    spot = (
        lax.broadcasted_iota(jnp.int32, (8, LANES), 0)
        == lax.broadcasted_iota(jnp.int32, (8, LANES), 1)
    )
    cot_row = jnp.sum(jnp.where(spot, cot_sum[...], 0.0), axis=0, keepdims=True)
    lane = lax.broadcasted_iota(jnp.int32, (1, LANES), 1)
    for h in range(2):
        line = cot_row if h == 0 else pltpu.roll(cot_row, LANES - 4, 1)
        line = jnp.where(lane < 4, line, 0.0)
        line = jnp.concatenate([line, jnp.zeros((1, NET_WIDTH - LANES), F32)], axis=1)
        grad[h, HEAD_ROW : HEAD_ROW + 16, :] = jnp.concatenate(
            [hidden[h][4 * h : 4 * h + 4], codes[4 * h : 4 * h + 4], line]
            + bias[h]
            + [jnp.zeros((7 - LAYERS, NET_WIDTH), F32)],
            axis=0,
        )

    for layer in reversed(range(LAYERS)):
        first = 0 if layer == 0 else ENC_WIDTH + (layer - 1) * NET_WIDTH
        for h in range(2):
            if layer == 0:
                value = dot(arr[...], pre[0, h], TN)
                grad[h, 0:ENC_WIDTH, :] = value[ENC_WIDTH * h : ENC_WIDTH * (h + 1)]
            else:
                grad[h, first : first + NET_WIDTH, :] = dot(act[layer - 1, h], pre[layer, h], TN)
        near_copy(layer).start()
        if layer < top:
            second_stage(layer + 1)
        if layer < top - 1:
            third_stage(layer + 2)
    second_stage(0)
    third_stage(1)
    third_stage(0)
    for layer in reversed(range(LAYERS)):
        near_copy(layer).wait_send()
        far_copy(layer).wait_send()
        full_copy(layer).wait_send()
        other = pltpu.make_async_remote_copy(
            full.at[1 - core, chunks[layer]], full.at[1 - core, chunks[layer]],
            s2.at[2, layer], r2.at[2, layer], device_id={"dp": near}, device_id_type=MESH,
        )
        other.wait_recv()
        grad_out[:, chunks[layer], :] = full[:, chunks[layer], :]


def shards(
    features, spacing, targets, ray_length, cell_id, slot_rank, image_id,
    params, first_moment, second_moment, code_table, table_first, table_second,
):
    ray_rows = features.shape[0]
    sample_count = ray_rows * SAMPLES
    groups = lax.axis_size("expert")
    experts_all = params.shape[0] * groups
    cap = 2 * (sample_count * 3 // 4 // experts_all)
    cap_up = -(-cap // LANES) * LANES
    width = cap_up + LANES
    slots_up = experts_all * cap_up
    table_rows = code_table.shape[0]
    block_index = lax.axis_index("expert") * lax.axis_size("dp") + lax.axis_index("dp")
    local_image = (image_id - block_index * table_rows)[None, :]
    cell = cell_id.T
    rank = slot_rank.T
    slot = jnp.where(rank >= 0, cell * cap_up + rank, slots_up).reshape(sample_count)
    weights_bf = params.astype(BF16)
    queries = weights_bf[:, HEAD_ROW + 4 : HEAD_ROW + 8, :CODE_WIDTH].reshape(8, CODE_WIDTH)
    shift = weights_bf[:, HEAD_ROW + 8, :4].reshape(8, 1)
    tail_msg = jnp.pad(
        jnp.concatenate([queries, shift], axis=1).astype(F32),
        ((0, 0), (0, LANES - CODE_WIDTH - 1)),
    )
    shape = jax.ShapeDtypeStruct
    big = 60 * 2**20
    table_scratch = pltpu.VMEM((slots_up + 8, LANES), F32)
    rows_scratch = pltpu.VMEM((sample_count, LANES), F32)
    msg_shape = (groups, 8, width)
    disp = pl.pallas_call(
        functools.partial(place_kernel, groups, cap, cap_up),
        out_shape=shape((groups, cap, LANES), BF16),
        in_specs=[SMEM, VMEM],
        out_specs=VMEM,
        scratch_shapes=[rows_scratch, table_scratch],
        compiler_params=pltpu.CompilerParams(vmem_limit_bytes=32 * 2**20),
        name="place",
    )(slot, features.transpose(1, 2, 0))
    sems = pltpu.SemaphoreType.DMA((groups,))
    arr, raw_back = pl.pallas_call(
        functools.partial(forward_kernel, groups, cap, cap_up),
        out_shape=(shape((groups, cap, LANES), BF16), shape(msg_shape, F32)),
        in_specs=[VMEM] * 3,
        out_specs=(VMEM, VMEM),
        scratch_shapes=[
            pltpu.VMEM((groups, cap, LANES), BF16),
            pltpu.VMEM(msg_shape, F32),
            pltpu.VMEM(msg_shape, F32),
            pltpu.VMEM((2, LANES, NET_WIDTH), BF16),
            sems, sems, sems, sems,
        ],
        compiler_params=pltpu.CompilerParams(
            collective_id=0, has_side_effects=True, vmem_limit_bytes=32 * 2**20
        ),
        name="dispatch",
    )(disp, weights_bf, tail_msg)
    table_shape = shape(code_table.shape, F32)
    loss, cot_msg, new_table, new_table_first, new_table_second = pl.pallas_call(
        functools.partial(home_kernel, groups, cap_up),
        out_shape=(
            shape((1, ray_rows), F32), shape(msg_shape, F32), table_shape, table_shape, table_shape,
        ),
        in_specs=[SMEM] + [VMEM] * 9,
        out_specs=(VMEM,) * 5,
        scratch_shapes=[
            rows_scratch,
            table_scratch,
            pltpu.VMEM((8 * SAMPLES, LANES), F32),
            pltpu.VMEM((8 * groups, LANES), F32),
            pltpu.VMEM((8 * groups, CODE_WIDTH), F32),
            pltpu.VMEM((8 * groups, LANES), F32),
        ],
        compiler_params=pltpu.CompilerParams(vmem_limit_bytes=32 * 2**20),
        name="home",
    )(
        slot, raw_back, cell, spacing.T, ray_length[None, :], targets, local_image,
        code_table, table_first, table_second,
    )
    all_rows = groups * cap
    grad_rows = params.shape[1]
    param_grad = pl.pallas_call(
        functools.partial(backward_kernel, groups, cap, cap_up),
        out_shape=shape(params.shape, F32),
        in_specs=[VMEM] * 3,
        out_specs=VMEM,
        scratch_shapes=[
            pltpu.VMEM(msg_shape, F32),
            pltpu.VMEM((LAYERS, 2, all_rows, NET_WIDTH), BF16),
            pltpu.VMEM((LAYERS, 2, all_rows, NET_WIDTH), BF16),
            pltpu.VMEM((2, LANES, NET_WIDTH), BF16),
            pltpu.VMEM((2, 8, NET_WIDTH), F32),
            pltpu.VMEM((8, LANES), F32),
            pltpu.VMEM((8, LANES), F32),
            pltpu.VMEM((2, grad_rows, NET_WIDTH), F32),
            pltpu.VMEM((grad_rows, NET_WIDTH), F32),
            pltpu.VMEM((grad_rows, NET_WIDTH), BF16),
            pltpu.VMEM((grad_rows, NET_WIDTH), BF16),
            pltpu.VMEM((2, grad_rows, NET_WIDTH), F32),
            sems, sems,
            pltpu.SemaphoreType.DMA((3, LAYERS)),
            pltpu.SemaphoreType.DMA((3, LAYERS)),
        ],
        compiler_params=pltpu.CompilerParams(
            collective_id=1, has_side_effects=True, vmem_limit_bytes=big
        ),
        name="backward",
    )(cot_msg, weights_bf, arr.reshape(all_rows, LANES))
    new_params, new_first, new_second = adam_update(params, param_grad, first_moment, second_moment)
    return (
        loss.reshape(ray_rows), new_params, new_first, new_second,
        new_table, new_table_first, new_table_second,
    )


def solution(mesh):
    both = ("expert", "dp")
    return jax.shard_map(
        shards,
        mesh=mesh,
        in_specs=(
            P(both, None, None), P(both, None), P(None, both), P(both), P(both, None),
            P(both, None), P(both),
            P("expert", None, None), P("expert", None, None), P("expert", None, None),
            P(both, None), P(both, None), P(both, None),
        ),
        out_specs=(
            P(both),
            P("expert", None, None), P("expert", None, None), P("expert", None, None),
            P(both, None), P(both, None), P(both, None),
        ),
        check_vma=False,
    )
```

time: 291 us -> 112 us (0.38); the launches traced: 287 us -> 111 us
  Pallas kernels: 0 us -> 99.3 us
  waiting for transfers between devices: 89.3 us -> 0 us
  local copies, waits for them, and re-layouts: 91.2 us -> 2.74 us
  matrix products: 40.9 us -> 0 us
  other arithmetic: 25.4 us -> 8.53 us
  starting transfers between devices: 15.6 us -> 0 us
  between operations: 14.9 us -> 0.78 us
  blocking collectives: 9.38 us -> 0 us
    pallas_call x0 -> x4, Pallas kernels: none -> 99.3 us  [the longest x1 37.7 us: shards(): pl.pallas_call(functools.partial(backward_kernel, groups, cap, cap_up), o...]
    psum x1 -> x0, waiting for transfers between devices: 46.4 us -> none  [shards(): param_grad = lax.psum(local_grad, 'dp')]
    all_to_all x3 -> x0, waiting for transfers between devices: 42.9 us -> none  [the longest x1 35.9 us: shards(): lax.all_to_all(outgoing, 'expert', split_axis=0, concat_axis=1, tiled=True)]
    dot_general x19 -> x0, matrix products: 40.9 us -> none  [the longest x4 13.4 us: hidden_pass(): jnp.einsum('enr,erw->enw', current, matrix, preferred_element_type=jnp.fl...]
    gather x3 -> x0, local copies, waits for them, and re-layouts: 30.4 us -> none  [pick_rows(): return jnp.take(buffer, slot_index, axis=0, mode='fill', fill_value=0)]
    unnamed x66 -> x24, local copies, waits for them, and re-layouts: 18.5 us -> 2.62 us
    all_to_all x3 -> x0, starting transfers between devices: 15.3 us -> none  [the longest x1 7.83 us: shards(): lax.all_to_all(outgoing, 'expert', split_axis=0, concat_axis=1, tiled=True)]
    scatter x1 -> x0, other arithmetic: 13.5 us -> none  [place_rows(): return blank.at[slot_index].set(rows, mode='drop')]
  transfers between devices with their start and end apart: 4 -> 0, of which waited for: 3 -> 0; matrix products, arithmetic and copies ran while one was open for 8% -> 0% of each run, Pallas kernels for 0% -> 0%
where the time goes in v1:
time: 112 us; the launch traced here: 111 us
  Pallas kernels  99.3 us (89%)
  other arithmetic  8.53 us (8%)
  local copies, waits for them, and re-layouts  2.74 us (2%)
    pallas_call x1, Pallas kernels, shards(): pl.pallas_call(functools.partial(backward_kernel, groups, cap, cap_up), o...  37.7 us
    pallas_call x1, Pallas kernels, shards(): pl.pallas_call(functools.partial(forward_kernel, groups, cap, cap_up), ou...  35.1 us
    pallas_call x1, Pallas kernels, shards(): pl.pallas_call(functools.partial(home_kernel, groups, cap_up), out_shape=...  18.3 us
    pallas_call x1, Pallas kernels, shards(): pl.pallas_call(functools.partial(place_kernel, groups, cap, cap_up), out_...  8.24 us
    sub x1, other arithmetic, adam_update(): return (param_now - update, new_one, new_two)  5.48 us
    unnamed x24, local copies, waits for them, and re-layouts  2.62 us

profile of v1, /device:TPU:0, one launch (start us, length us, event | category | flops | bytes accessed | tf_op | source)
XLA Modules:
  0.0 111.4 jit_solution(5787915867025490238)
XLA Ops:
  0.6 0.7 subtract_bitcast_fusion.image_ref
  1.3 0.7 fusion.2.slot_ref
  2.0 0.0 copy-start.2
  2.0 1.0 copy-done.2
  3.1 8.2 %place.1.disp = bf16[8,384,128]{2,1,0:T(8,128)(2,1)S(1)} custom-call(s32[4096]{0:T(1024)S(1)} %fusion.2.slot_ref, bf16[32,64,128]{2,1,0:T(8,128)(2,1)S(1)} %bitcast.22), custom_call_target="tpu_custom_call" | custom-call | tf_op jit(solution)/shard_map/place/pallas_call | solution.py:534
  11.3 0.0 copy-start.4
  11.3 0.0 copy-start.5
  11.4 0.0 copy-start.6
  11.4 0.0 copy-start.7
  11.4 0.0 copy-start.8
  11.4 0.0 copy-start.9
  11.4 0.0 copy-start.10
  11.4 1.6 %convert_element_type.6.wt = bf16[2,848,256]{2,1,0:T(8,128)(2,1)S(1)} convert(f32[2,848,256]{2,1,0:T(8,128)} %param.20) | non-fusion elementwise | flops 434176 | bytes 2605056 | tf_op jit(solution)/shard_map/convert_element_type | solution.py:522
  13.0 0.0 copy-start
  13.0 0.1 reshape_squeeze.4
  13.1 0.1 fusion.6.tail_msg
  13.2 35.1 %dispatch.1 = (bf16[8,384,128]{2,1,0:T(8,128)(2,1)S(1)}, f32[8,8,512]{2,1,0:T(8,128)S(1)}) custom-call(bf16[8,384,128]{2,1,0:T(8,128)(2,1)S(1)} %place.1.disp, bf16[2,848,256]{2,1,0:T(8,128)(2,1)S(1)} %convert_element_type.6.wt, f32[8,128]{1,0:T(8,128)S(1)} %fusion.6.tail_msg), custom_call_target="tpu_custom_call" | custom-call | tf_op jit(solution)/shard_map/dispatch/pallas_call | solution.py:544
  48.3 0.0 copy-start.1
  48.3 0.9 copy-done.1
  49.2 0.0 copy-done.4
  49.2 0.0 copy-done.5
  49.2 0.0 copy-done.6
  49.2 0.0 copy-done.7
  49.2 0.0 copy-done.8
  49.2 0.0 copy-done.9
  49.2 0.0 copy-done.10
  49.2 18.3 %home.1 = (f32[1,128]{1,0:T(1,128)}, f32[8,8,512]{2,1,0:T(8,128)S(1)}, f32[16,64]{1,0:T(8,128)}, f32[16,64]{1,0:T(8,128)}, f32[16,64]{1,0:T(8,128)}) custom-call(s32[4096]{0:T(1024)S(1)} %fusion.2.slot_ref, f32[8,8,512]{2,1,0:T(8,128)S(1)} %get-tuple-element.14.raw_ref, s32[32,128]{1,0:T(8,128)S(1)} %bitcast.23, f32[32,128]{1,0:T(8,128)S(1)} %bitcast.24, ...), custom_call_target="tpu_custom_call" | custom-call | tf_op jit(solution)/shard_map/home/pallas_call | solution.py:562
  67.5 0.7 copy-done.3
  68.2 0.0 copy-done
  68.2 37.7 %backward.1 = f32[2,848,256]{2,1,0:T(8,128)} custom-call(f32[8,8,512]{2,1,0:T(8,128)} %copy-done.3, bf16[2,848,256]{2,1,0:T(8,128)(2,1)} %copy-done, bf16[3072,128]{1,0:T(8,128)(2,1)} %bitcast.21), custom_call_target="tpu_custom_call" | custom-call | tf_op jit(solution)/shard_map/backward/pallas_call | solution.py:585
  105.9 0.0 copy-done.11
  105.9 5.5 %divide_subtract_fusion = (f32[2,848,256]{2,1,0:T(8,128)}, f32[2,848,256]{2,1,0:T(8,128)}, f32[2,848,256]{2,1,0:T(8,128)}) fusion(f32[2,848,256]{2,1,0:T(8,128)S(1)} %copy-done.11, f32[2,848,256]{2,1,0:T(8,128)} %backward.1, f32[2,848,256]{2,1,0:T(8,128)} %param.21, f32[2,848,256]{2,1,0:T(8,128)} %param.22), kind=kLoop, calls=%fused_computation.2 | loop fusion | flops 5210112 | bytes 12156928 | tf_op jit(solution)/shard_map/sub | solution.py:47
  (4 shorter events, 0.0 us)
Async XLA Ops:
  2.0 1.0 copy-start.2
  11.3 37.9 %copy-start.4 = (s32[128,32]{0,1:T(8,128)S(1)}, s32[128,32]{0,1:T(8,128)}, u32[]{:S(2)}) copy-start(s32[128,32]{0,1:T(8,128)} %param.17) | copy-start | bytes 49156
  11.3 37.9 %copy-start.5 = (f32[128,32]{0,1:T(8,128)S(1)}, f32[128,32]{0,1:T(8,128)}, u32[]{:S(2)}) copy-start(f32[128,32]{0,1:T(8,128)} %param.14) | copy-start | bytes 49156
  11.4 37.9 %copy-start.6 = (f32[16,64]{1,0:T(8,128)S(1)}, f32[16,64]{1,0:T(8,128)}, u32[]{:S(2)}) copy-start(f32[16,64]{1,0:T(8,128)} %code_ref.1) | copy-start | bytes 12292
  11.4 37.8 %copy-start.7 = (f32[16,64]{1,0:T(8,128)S(1)}, f32[16,64]{1,0:T(8,128)}, u32[]{:S(2)}) copy-start(f32[16,64]{1,0:T(8,128)} %first_ref.1) | copy-start | bytes 12292
  11.4 37.8 %copy-start.8 = (f32[16,64]{1,0:T(8,128)S(1)}, f32[16,64]{1,0:T(8,128)}, u32[]{:S(2)}) copy-start(f32[16,64]{1,0:T(8,128)} %second_ref.1) | copy-start | bytes 12292
  11.4 37.8 %copy-start.9 = (f32[3,128]{1,0:T(4,128)S(1)}, f32[3,128]{1,0:T(4,128)}, u32[]{:S(2)}) copy-start(f32[3,128]{1,0:T(4,128)} %target_ref.1) | copy-start | bytes 4612
  11.4 37.8 %copy-start.10 = (s32[128]{0:T(128)S(1)}, s32[128]{0:T(128)}, u32[]{:S(2)}) copy-start(s32[128]{0:T(128)} %param.16) | copy-start | bytes 1540
  13.0 55.2 %copy-start = (bf16[2,848,256]{2,1,0:T(8,128)(2,1)}, bf16[2,848,256]{2,1,0:T(8,128)(2,1)S(1)}, u32[]{:S(2)}) copy-start(bf16[2,848,256]{2,1,0:T(8,128)(2,1)S(1)} %convert_element_type.6.wt) | copy-start | bytes 2605060
  48.3 0.9 copy-start.1
  67.5 0.7 copy-start.3
  68.2 37.7 %copy-start.11 = (f32[2,848,256]{2,1,0:T(8,128)S(1)}, f32[2,848,256]{2,1,0:T(8,128)}, u32[]{:S(2)}) copy-start(f32[2,848,256]{2,1,0:T(8,128)} %param.20) | copy-start | bytes 5210116

commit v2 on v1

--- a/solution.py
+++ b/solution.py
@@ -117,19 +117,22 @@
     return wt_ref[h, HEAD_ROW : HEAD_ROW + 16, :]
 
 
-def forward(wt_ref, m0, h, current, keep=None):
-    tail = tail_rows(wt_ref, h).astype(F32)
+def forward(wt_ref, m0, block, keep=None):
+    tails = [tail_rows(wt_ref, h).astype(F32) for h in range(2)]
+    current = [block, block]
     for layer in range(LAYERS):
-        preact = dot(current, layer_matrix(wt_ref, m0, h, layer))
-        preact = preact + tail[9 + layer : 10 + layer, :]
-        current = jnp.maximum(preact, 0.0).astype(BF16)
-        if keep is not None:
-            keep(layer, current)
+        for h in range(2):
+            preact = dot(current[h], layer_matrix(wt_ref, m0, h, layer))
+            preact = preact + tails[h][9 + layer : 10 + layer, :]
+            current[h] = jnp.maximum(preact, 0.0).astype(BF16)
+            if keep is not None:
+                keep(layer, h, current[h])
     return current
 
 
 def forward_kernel(
-    groups, cap, cap_up, disp, wt, tail_msg, arr, raw_out, recv, msg, back, m0, s1, r1, s2, r2
+    groups, cap, cap_up, disp, params, arr, raw_out, wt, recv, msg, back, m0, tail_msg,
+    s1, r1, s2, r2,
 ):
     me = lax.axis_index("expert")
     barrier = greet(groups, me)
@@ -154,16 +157,27 @@
         return carry
 
     lax.fori_loop(1, groups, start, 0)
+    wt[...] = params[...].astype(BF16)
     pad_first(wt, m0)
+    spot = lax.broadcasted_iota(jnp.int32, (4, LANES), 0) == lax.broadcasted_iota(
+        jnp.int32, (4, LANES), 1
+    )
+    lane = lax.broadcasted_iota(jnp.int32, (4, LANES), 1)
+    for h in range(2):
+        tail = tail_rows(wt, h).astype(F32)
+        column = jnp.sum(jnp.where(spot, tail[8:9, 0:LANES], 0.0), axis=1, keepdims=True)
+        tail_msg[4 * h : 4 * h + 4, :] = jnp.where(
+            lane < CODE_WIDTH, tail[4:8, 0:LANES], jnp.where(lane == CODE_WIDTH, column, 0.0)
+        )
 
     def process(k, block):
         arr[k] = block
         msg[k, :, cap_up:] = tail_msg[...]
         if cap_up > cap:
             msg[k, :, cap:cap_up] = jnp.zeros((8, cap_up - cap), F32)
+        acts = forward(wt, m0, block)
         for h in range(2):
-            act = forward(wt, m0, h, block)
-            raw = dot(tail_rows(wt, h), act, NT)
+            raw = dot(tail_rows(wt, h), acts[h], NT)
             msg[k, 4 * h : 4 * h + 4, 0:cap] = raw[0:4]
 
     process(0, disp[me])
@@ -329,8 +343,8 @@
 
 
 def backward_kernel(
-    groups, cap, cap_up, msg, wt, arr, grad_out, recv, act, pre, m0, head, code_sum, cot_sum,
-    grad, half_in, sum_out, sum_in, full, s1, r1, s2, r2,
+    groups, cap, cap_up, msg, wt, arr, grad_out, recv, act, pre, m0, turned, head, code_sum,
+    cot_sum, bias, grad, half_in, sum_out, sum_in, full, s1, r1, s2, r2,
 ):
     me = lax.axis_index("expert")
     my_dp = lax.axis_index("dp")
@@ -356,20 +370,29 @@
     lax.fori_loop(1, groups, start, 0)
     pad_first(wt, m0)
     head[...] = jnp.zeros_like(head)
+    bias[...] = jnp.zeros_like(bias)
     for h in range(2):
         head[h, 4 * h : 4 * h + 4, :] = tail_rows(wt, h).astype(F32)[0:4]
-
-    def again(k, carry):
-        block = pl.ds(pl.multiple_of(k * cap, 16), cap)
-        for h in range(2):
-
-            def keep(layer, value):
-                act[layer, h, block, :] = value
-
-            forward(wt, m0, h, arr[block, :], keep)
-        return carry
-
-    lax.fori_loop(0, groups, again, 0)
+        for layer in range(1, LAYERS):
+            matrix = layer_matrix(wt, m0, h, layer)
+            turned[layer - 1, h] = matrix.astype(F32).T.astype(BF16)
+
+    pieces = 4
+    size = arr.shape[0] // pieces
+
+    def piece(index):
+        return pl.ds(pl.multiple_of(index * size, 16), size)
+
+    def again(index, carry):
+        block = piece(index)
+
+        def keep(layer, h, value):
+            act[layer, h, block, :] = value
+
+        forward(wt, m0, arr[block, :], keep)
+        return carry
+
+    lax.fori_loop(0, pieces, again, 0)
     recv[0] = msg[me]
 
     def arrive(k, carry):
@@ -378,83 +401,93 @@
 
     lax.fori_loop(1, groups, arrive, 0)
 
-    chunks = []
-    for layer in range(LAYERS):
-        first = 0 if layer == 0 else ENC_WIDTH + (layer - 1) * NET_WIDTH
-        last = HEAD_ROW + 16 if layer == LAYERS - 1 else ENC_WIDTH + layer * NET_WIDTH
-        chunks.append(pl.ds(first, last - first))
-
-    def near_copy(layer):
+    starts = [0] + [ENC_WIDTH + layer * NET_WIDTH for layer in range(LAYERS)] + [HEAD_ROW + 16]
+    chunks = [pl.ds(starts[j], starts[j + 1] - starts[j]) for j in range(LAYERS + 1)]
+
+    def near_copy(j):
         return pltpu.make_async_remote_copy(
-            grad.at[1 - core, chunks[layer]], half_in.at[chunks[layer]],
-            s2.at[0, layer], r2.at[0, layer], device_id={"dp": near}, device_id_type=MESH,
-        )
-
-    def far_copy(layer):
+            grad.at[1 - core, chunks[j]], half_in.at[chunks[j]],
+            s2.at[0, j], r2.at[0, j], device_id={"dp": near}, device_id_type=MESH,
+        )
+
+    def far_copy(j):
         return pltpu.make_async_remote_copy(
-            sum_out.at[chunks[layer]], sum_in.at[chunks[layer]],
-            s2.at[1, layer], r2.at[1, layer], device_id={"dp": far}, device_id_type=MESH,
-        )
-
-    def full_copy(layer):
+            sum_out.at[chunks[j]], sum_in.at[chunks[j]],
+            s2.at[1, j], r2.at[1, j], device_id={"dp": far}, device_id_type=MESH,
+        )
+
+    def full_copy(j, which):
         return pltpu.make_async_remote_copy(
-            full.at[core, chunks[layer]], full.at[core, chunks[layer]],
-            s2.at[2, layer], r2.at[2, layer], device_id={"dp": near}, device_id_type=MESH,
-        )
-
-    def second_stage(layer):
-        near_copy(layer).wait_recv()
-        rows = chunks[layer]
+            full.at[which, chunks[j]], full.at[which, chunks[j]],
+            s2.at[2, j], r2.at[2, j], device_id={"dp": near}, device_id_type=MESH,
+        )
+
+    def second_stage(j):
+        near_copy(j).wait_recv()
+        rows = chunks[j]
         sum_out[rows, :] = (grad[core, rows, :] + half_in[rows, :]).astype(BF16)
-        far_copy(layer).start()
-
-    def third_stage(layer):
-        far_copy(layer).wait_recv()
-        rows = chunks[layer]
+        far_copy(j).start()
+
+    def third_stage(j):
+        far_copy(j).wait_recv()
+        rows = chunks[j]
         full[core, rows, :] = sum_out[rows, :].astype(F32) + sum_in[rows, :].astype(F32)
-        full_copy(layer).start()
-
-    bias = [[None] * LAYERS for _ in range(2)]
+        full_copy(j, core).start()
+
     top = LAYERS - 1
-    hidden = []
-
-    for h in range(2):
-
-        def back(k, carry):
-            block = pl.ds(pl.multiple_of(k * cap, 16), cap)
-            cot = recv[k, :, 0:cap].astype(BF16)
-            up = dot(cot, head[h].astype(BF16), TN)
-            sums = []
-            for layer in reversed(range(LAYERS)):
-                value = jnp.where(act[layer, h, block, :].astype(F32) > 0, up, 0.0).astype(BF16)
-                pre[layer, h, block, :] = value
-                sums.append(
-                    carry[top - layer] + jnp.sum(value.astype(F32), axis=0, keepdims=True)
-                )
-                if layer > 0:
-                    up = dot(value, layer_matrix(wt, m0, h, layer), NT)
-            heads = carry[LAYERS] + dot(cot, act[top, h, block, :])
-            return tuple(sums) + (heads,)
-
-        zero = jnp.zeros((1, NET_WIDTH), F32)
-        done = lax.fori_loop(
-            0, groups, back, (zero,) * LAYERS + (jnp.zeros((8, NET_WIDTH), F32),)
-        )
-        for layer in range(LAYERS):
-            bias[h][layer] = done[top - layer]
-        hidden.append(done[LAYERS])
+    heads_bf = [head[h].astype(BF16) for h in range(2)]
+
+    def mask_store(layer, h, block, up):
+        value = jnp.where(act[layer, h, block, :].astype(F32) > 0, up, 0.0).astype(BF16)
+        pre[layer, h, block, :] = value
+        bias[layer, h] += jnp.sum(
+            value.astype(F32).reshape(-1, 8, NET_WIDTH), axis=0
+        )
 
     code_sum[...] = jnp.zeros_like(code_sum)
     cot_sum[...] = jnp.zeros_like(cot_sum)
 
-    def add_codes(k, carry):
+    def first_back(k, carry):
+        block = pl.ds(pl.multiple_of(k * cap, 16), cap)
+        cot = recv[k, :, 0:cap].astype(BF16)
+        sums = []
+        for h in range(2):
+            mask_store(top, h, block, dot(cot, heads_bf[h], TN))
+            sums.append(carry[h] + dot(cot, act[top, h, block, :]))
         code_sum[...] += recv[k, :, cap_up:]
         cot_sum[...] += jnp.broadcast_to(
             jnp.sum(recv[k, :, 0:cap], axis=1, keepdims=True), (8, LANES)
         )
-        return carry
-
-    lax.fori_loop(0, groups, add_codes, 0)
+        return tuple(sums)
+
+    hidden = lax.fori_loop(
+        0, groups, first_back, (jnp.zeros((8, NET_WIDTH), F32), jnp.zeros((8, NET_WIDTH), F32))
+    )
+
+    for layer in reversed(range(LAYERS)):
+        if layer < top:
+
+            def back(index, carry):
+                block = piece(index)
+                for h in range(2):
+                    mask_store(
+                        layer, h, block, dot(pre[layer + 1, h, block, :], turned[layer, h])
+                    )
+                return carry
+
+            lax.fori_loop(0, pieces, back, 0)
+        for h in range(2):
+            if layer == 0:
+                value = dot(arr[...], pre[0, h], TN)
+                grad[h, 0:ENC_WIDTH, :] = value[ENC_WIDTH * h : ENC_WIDTH * (h + 1)]
+            else:
+                grad[h, chunks[layer], :] = dot(act[layer - 1, h], pre[layer, h], TN)
+        near_copy(layer).start()
+        if layer < top:
+            second_stage(layer + 1)
+        if layer < top - 1:
+            third_stage(layer + 2)
+
     codes = jnp.concatenate([code_sum[...], jnp.zeros((8, NET_WIDTH - LANES), F32)], axis=1)
     spot = (
         lax.broadcasted_iota(jnp.int32, (8, LANES), 0)
@@ -468,37 +501,22 @@
         line = jnp.concatenate([line, jnp.zeros((1, NET_WIDTH - LANES), F32)], axis=1)
         grad[h, HEAD_ROW : HEAD_ROW + 16, :] = jnp.concatenate(
             [hidden[h][4 * h : 4 * h + 4], codes[4 * h : 4 * h + 4], line]
-            + bias[h]
+            + [jnp.sum(bias[layer, h], axis=0, keepdims=True) for layer in range(LAYERS)]
             + [jnp.zeros((7 - LAYERS, NET_WIDTH), F32)],
             axis=0,
         )
-
-    for layer in reversed(range(LAYERS)):
-        first = 0 if layer == 0 else ENC_WIDTH + (layer - 1) * NET_WIDTH
-        for h in range(2):
-            if layer == 0:
-                value = dot(arr[...], pre[0, h], TN)
-                grad[h, 0:ENC_WIDTH, :] = value[ENC_WIDTH * h : ENC_WIDTH * (h + 1)]
-            else:
-                grad[h, first : first + NET_WIDTH, :] = dot(act[layer - 1, h], pre[layer, h], TN)
-        near_copy(layer).start()
-        if layer < top:
-            second_stage(layer + 1)
-        if layer < top - 1:
-            third_stage(layer + 2)
+    near_copy(LAYERS).start()
     second_stage(0)
     third_stage(1)
+    second_stage(LAYERS)
     third_stage(0)
-    for layer in reversed(range(LAYERS)):
-        near_copy(layer).wait_send()
-        far_copy(layer).wait_send()
-        full_copy(layer).wait_send()
-        other = pltpu.make_async_remote_copy(
-            full.at[1 - core, chunks[layer]], full.at[1 - core, chunks[layer]],
-            s2.at[2, layer], r2.at[2, layer], device_id={"dp": near}, device_id_type=MESH,
-        )
-        other.wait_recv()
-        grad_out[:, chunks[layer], :] = full[:, chunks[layer], :]
+    third_stage(LAYERS)
+    for j in (3, 2, 1, 0, LAYERS):
+        near_copy(j).wait_send()
+        far_copy(j).wait_send()
+        full_copy(j, core).wait_send()
+        full_copy(j, 1 - core).wait_recv()
+        grad_out[:, chunks[j], :] = full[:, chunks[j], :]
 
 
 def shards(
@@ -519,15 +537,8 @@
     cell = cell_id.T
     rank = slot_rank.T
     slot = jnp.where(rank >= 0, cell * cap_up + rank, slots_up).reshape(sample_count)
-    weights_bf = params.astype(BF16)
-    queries = weights_bf[:, HEAD_ROW + 4 : HEAD_ROW + 8, :CODE_WIDTH].reshape(8, CODE_WIDTH)
-    shift = weights_bf[:, HEAD_ROW + 8, :4].reshape(8, 1)
-    tail_msg = jnp.pad(
-        jnp.concatenate([queries, shift], axis=1).astype(F32),
-        ((0, 0), (0, LANES - CODE_WIDTH - 1)),
-    )
     shape = jax.ShapeDtypeStruct
-    big = 60 * 2**20
+    big = 46 * 2**20
     table_scratch = pltpu.VMEM((slots_up + 8, LANES), F32)
     rows_scratch = pltpu.VMEM((sample_count, LANES), F32)
     msg_shape = (groups, 8, width)
@@ -541,23 +552,26 @@
         name="place",
     )(slot, features.transpose(1, 2, 0))
     sems = pltpu.SemaphoreType.DMA((groups,))
-    arr, raw_back = pl.pallas_call(
+    arr, raw_back, weights_bf = pl.pallas_call(
         functools.partial(forward_kernel, groups, cap, cap_up),
-        out_shape=(shape((groups, cap, LANES), BF16), shape(msg_shape, F32)),
-        in_specs=[VMEM] * 3,
-        out_specs=(VMEM, VMEM),
+        out_shape=(
+            shape((groups, cap, LANES), BF16), shape(msg_shape, F32), shape(params.shape, BF16),
+        ),
+        in_specs=[VMEM] * 2,
+        out_specs=(VMEM,) * 3,
         scratch_shapes=[
             pltpu.VMEM((groups, cap, LANES), BF16),
             pltpu.VMEM(msg_shape, F32),
             pltpu.VMEM(msg_shape, F32),
             pltpu.VMEM((2, LANES, NET_WIDTH), BF16),
+            pltpu.VMEM((8, LANES), F32),
             sems, sems, sems, sems,
         ],
         compiler_params=pltpu.CompilerParams(
             collective_id=0, has_side_effects=True, vmem_limit_bytes=32 * 2**20
         ),
         name="dispatch",
-    )(disp, weights_bf, tail_msg)
+    )(disp, params)
     table_shape = shape(code_table.shape, F32)
     loss, cot_msg, new_table, new_table_first, new_table_second = pl.pallas_call(
         functools.partial(home_kernel, groups, cap_up),
@@ -592,17 +606,19 @@
             pltpu.VMEM((LAYERS, 2, all_rows, NET_WIDTH), BF16),
             pltpu.VMEM((LAYERS, 2, all_rows, NET_WIDTH), BF16),
             pltpu.VMEM((2, LANES, NET_WIDTH), BF16),
+            pltpu.VMEM((LAYERS - 1, 2, NET_WIDTH, NET_WIDTH), BF16),
             pltpu.VMEM((2, 8, NET_WIDTH), F32),
             pltpu.VMEM((8, LANES), F32),
             pltpu.VMEM((8, LANES), F32),
+            pltpu.VMEM((LAYERS, 2, 8, NET_WIDTH), F32),
             pltpu.VMEM((2, grad_rows, NET_WIDTH), F32),
             pltpu.VMEM((grad_rows, NET_WIDTH), F32),
             pltpu.VMEM((grad_rows, NET_WIDTH), BF16),
             pltpu.VMEM((grad_rows, NET_WIDTH), BF16),
             pltpu.VMEM((2, grad_rows, NET_WIDTH), F32),
             sems, sems,
-            pltpu.SemaphoreType.DMA((3, LAYERS)),
-            pltpu.SemaphoreType.DMA((3, LAYERS)),
+            pltpu.SemaphoreType.DMA((3, LAYERS + 1)),
+            pltpu.SemaphoreType.DMA((3, LAYERS + 1)),
         ],
         compiler_params=pltpu.CompilerParams(
             collective_id=1, has_side_effects=True, vmem_limit_bytes=big

time: 112 us -> 97 us (0.87)
  Pallas kernels: 99.3 us -> 89 us
  other arithmetic: 8.53 us -> 4.38 us
    pallas_call x1, Pallas kernels: 37.7 us -> 28.9 us  [shards(): pl.pallas_call(functools.partial(backward_kernel, groups, cap, cap_up), o...]
    sub x1, other arithmetic: 5.48 us -> 2.98 us  [adam_update(): return (param_now - update, new_one, new_two)]
    convert_element_type x1 -> x0, other arithmetic: 1.58 us -> none  [shards(): weights_bf = params.astype(BF16)]
    pallas_call x1, Pallas kernels: 35.1 us -> 33.6 us  [shards(): pl.pallas_call(functools.partial(forward_kernel, groups, cap, cap_up), ou...]
where the time goes in v2:
time: 97 us; the launch traced here: 96.7 us
  Pallas kernels  89 us (92%)
  other arithmetic  4.38 us (5%)
  local copies, waits for them, and re-layouts  2.55 us (3%)
    pallas_call x1, Pallas kernels, shards(): pl.pallas_call(functools.partial(forward_kernel, groups, cap, cap_up), ou...  33.6 us
    pallas_call x1, Pallas kernels, shards(): pl.pallas_call(functools.partial(backward_kernel, groups, cap, cap_up), o...  28.9 us
    pallas_call x1, Pallas kernels, shards(): pl.pallas_call(functools.partial(home_kernel, groups, cap_up), out_shape=...  18.3 us
    pallas_call x1, Pallas kernels, shards(): pl.pallas_call(functools.partial(place_kernel, groups, cap, cap_up), out_...  8.25 us
    sub x1, other arithmetic, adam_update(): return (param_now - update, new_one, new_two)  2.98 us
    unnamed x24, local copies, waits for them, and re-layouts  2.55 us

profile of v2, /device:TPU:0, one launch (start us, length us, event | category | flops | bytes accessed | tf_op | source)
XLA Modules:
  0.0 96.7 jit_solution(3522227064159843151)
XLA Ops:
  0.6 0.7 subtract_bitcast_fusion.image_ref
  1.3 0.7 fusion.2.slot_ref
  2.0 0.0 copy-start.2
  2.0 1.0 %copy-done.2 = bf16[128,32,64]{0,2,1:T(8,128)(2,1)S(1)} copy-done((bf16[128,32,64]{0,2,1:T(8,128)(2,1)S(1)}, bf16[128,32,64]{0,2,1:T(8,128)(2,1)}, u32[]{:S(2)}) %copy-start.2) | copy-done | bytes 524312
  3.1 0.0 copy-start.3
  3.1 0.0 copy-start.4
  3.1 0.0 copy-start.5
  3.1 0.0 copy-start.6
  3.1 0.0 copy-start.7
  3.1 0.0 copy-start.8
  3.1 0.0 copy-start.9
  3.1 8.2 %place.1.disp = bf16[8,384,128]{2,1,0:T(8,128)(2,1)S(1)} custom-call(s32[4096]{0:T(1024)S(1)} %fusion.2.slot_ref, bf16[32,64,128]{2,1,0:T(8,128)(2,1)S(1)} %bitcast.21), custom_call_target="tpu_custom_call" | custom-call | tf_op jit(solution)/shard_map/place/pallas_call | solution.py:545
  11.4 0.0 copy-start
  11.4 1.5 %copy-done = f32[2,848,256]{2,1,0:T(8,128)S(1)} copy-done((f32[2,848,256]{2,1,0:T(8,128)S(1)}, f32[2,848,256]{2,1,0:T(8,128)}, u32[]{:S(2)}) %copy-start) | copy-done | bytes 1736728
  12.8 0.0 copy-start.11
  12.9 33.6 %dispatch.1 = (bf16[8,384,128]{2,1,0:T(8,128)(2,1)S(1)}, f32[8,8,512]{2,1,0:T(8,128)S(1)}, bf16[2,848,256]{2,1,0:T(8,128)(2,1)S(1)}) custom-call(bf16[8,384,128]{2,1,0:T(8,128)(2,1)S(1)} %place.1.disp, f32[2,848,256]{2,1,0:T(8,128)S(1)} %copy-done), custom_call_target="tpu_custom_call" | custom-call | tf_op jit(solution)/shard_map/dispatch/pallas_call | solution.py:555
  46.4 0.0 copy-done.3
  46.4 0.0 copy-done.4
  46.5 0.0 copy-done.5
  46.5 0.0 copy-done.6
  46.5 0.0 copy-done.7
  46.5 0.0 copy-done.8
  46.5 0.0 copy-done.9
  46.5 18.3 %home.1 = (f32[1,128]{1,0:T(1,128)}, f32[8,8,512]{2,1,0:T(8,128)S(1)}, f32[16,64]{1,0:T(8,128)}, f32[16,64]{1,0:T(8,128)}, f32[16,64]{1,0:T(8,128)}) custom-call(s32[4096]{0:T(1024)S(1)} %fusion.2.slot_ref, f32[8,8,512]{2,1,0:T(8,128)S(1)} %get-tuple-element.15.raw_ref, s32[32,128]{1,0:T(8,128)S(1)} %bitcast.22, f32[32,128]{1,0:T(8,128)S(1)} %bitcast.23, ...), custom_call_target="tpu_custom_call" | custom-call | tf_op jit(solution)/shard_map/home/pallas_call | solution.py:576
  64.8 0.0 copy-start.1
  64.8 0.0 copy-start.10
  64.8 28.9 %backward.1 = f32[2,848,256]{2,1,0:T(8,128)S(1)} custom-call(f32[8,8,512]{2,1,0:T(8,128)S(1)} %get-tuple-element.17.msg, bf16[2,848,256]{2,1,0:T(8,128)(2,1)S(1)} %get-tuple-element.18.wt, bf16[3072,128]{1,0:T(8,128)(2,1)S(1)} %bitcast.20), custom_call_target="tpu_custom_call" | custom-call | tf_op jit(solution)/shard_map/backward/pallas_call | solution.py:599
  93.7 0.0 copy-done.11
  93.7 0.0 copy-done.1
  93.7 0.0 copy-done.10
  93.7 3.0 %divide_subtract_fusion = (f32[2,848,256]{2,1,0:T(8,128)}, f32[2,848,256]{2,1,0:T(8,128)}, f32[2,848,256]{2,1,0:T(8,128)}) fusion(f32[2,848,256]{2,1,0:T(8,128)S(1)} %copy-done.1, f32[2,848,256]{2,1,0:T(8,128)S(1)} %backward.1, f32[2,848,256]{2,1,0:T(8,128)S(1)} %copy-done.10, f32[2,848,256]{2,1,0:T(8,128)S(1)} %copy-done.11), kind=kLoop, calls=%fused_computation.2 | loop fusion | flops 5210112 | bytes 12156928 | tf_op jit(solution)/shard_map/sub | solution.py:47
Async XLA Ops:
  2.0 1.0 %copy-start.2 = (bf16[128,32,64]{0,2,1:T(8,128)(2,1)S(1)}, bf16[128,32,64]{0,2,1:T(8,128)(2,1)}, u32[]{:S(2)}) copy-start(bf16[128,32,64]{0,2,1:T(8,128)(2,1)} %param.13) | copy-start | bytes 1572868
  3.1 43.4 %copy-start.3 = (s32[128,32]{0,1:T(8,128)S(1)}, s32[128,32]{0,1:T(8,128)}, u32[]{:S(2)}) copy-start(s32[128,32]{0,1:T(8,128)} %param.17) | copy-start | bytes 49156
  3.1 43.4 %copy-start.4 = (f32[128,32]{0,1:T(8,128)S(1)}, f32[128,32]{0,1:T(8,128)}, u32[]{:S(2)}) copy-start(f32[128,32]{0,1:T(8,128)} %param.14) | copy-start | bytes 49156
  3.1 43.4 %copy-start.5 = (f32[16,64]{1,0:T(8,128)S(1)}, f32[16,64]{1,0:T(8,128)}, u32[]{:S(2)}) copy-start(f32[16,64]{1,0:T(8,128)} %code_ref.1) | copy-start | bytes 12292
  3.1 43.4 %copy-start.6 = (f32[16,64]{1,0:T(8,128)S(1)}, f32[16,64]{1,0:T(8,128)}, u32[]{:S(2)}) copy-start(f32[16,64]{1,0:T(8,128)} %first_ref.1) | copy-start | bytes 12292
  3.1 43.4 %copy-start.7 = (f32[16,64]{1,0:T(8,128)S(1)}, f32[16,64]{1,0:T(8,128)}, u32[]{:S(2)}) copy-start(f32[16,64]{1,0:T(8,128)} %second_ref.1) | copy-start | bytes 12292
  3.1 43.4 %copy-start.8 = (f32[3,128]{1,0:T(4,128)S(1)}, f32[3,128]{1,0:T(4,128)}, u32[]{:S(2)}) copy-start(f32[3,128]{1,0:T(4,128)} %target_ref.1) | copy-start | bytes 4612
  3.1 43.4 %copy-start.9 = (s32[128]{0:T(128)S(1)}, s32[128]{0:T(128)}, u32[]{:S(2)}) copy-start(s32[128]{0:T(128)} %param.16) | copy-start | bytes 1540
  11.4 1.5 %copy-start = (f32[2,848,256]{2,1,0:T(8,128)S(1)}, f32[2,848,256]{2,1,0:T(8,128)}, u32[]{:S(2)}) copy-start(f32[2,848,256]{2,1,0:T(8,128)} %params.1) | copy-start | bytes 5210116
  12.8 80.8 %copy-start.11 = (f32[2,848,256]{2,1,0:T(8,128)S(1)}, f32[2,848,256]{2,1,0:T(8,128)}, u32[]{:S(2)}) copy-start(f32[2,848,256]{2,1,0:T(8,128)} %param.22) | copy-start | bytes 5210116
  64.8 28.9 %copy-start.1 = (f32[2,848,256]{2,1,0:T(8,128)S(1)}, f32[2,848,256]{2,1,0:T(8,128)}, u32[]{:S(2)}) copy-start(f32[2,848,256]{2,1,0:T(8,128)} %params.1) | copy-start | bytes 5210116
  64.8 28.9 %copy-start.10 = (f32[2,848,256]{2,1,0:T(8,128)S(1)}, f32[2,848,256]{2,1,0:T(8,128)}, u32[]{:S(2)}) copy-start(f32[2,848,256]{2,1,0:T(8,128)} %param.21) | copy-start | bytes 5210116

commit v3 on v2

--- a/solution.py
+++ b/solution.py
@@ -52,7 +52,7 @@
 
 
 def move_rows(count, move):
-    step = 32
+    step = 128
 
     def body(block, carry):
         for inner in range(step):
@@ -62,15 +62,23 @@
     lax.fori_loop(0, count // step, body, 0)
 
 
+def unrolled(count, body, step=4):
+    def several(index, carry):
+        for inner in range(step):
+            body(index * step + inner)
+        return carry
+
+    lax.fori_loop(0, count // step, several, 0)
+
+
 def place_kernel(groups, cap, cap_up, slot_ref, feat_ref, out_ref, rows, table):
     table[...] = jnp.zeros_like(table)
 
-    def turn(i, carry):
+    def turn(i):
         block = feat_ref[i].astype(F32)
         rows[lane_block(i), :] = jnp.concatenate([block, block], axis=0).T
-        return carry
-
-    lax.fori_loop(0, SAMPLES, turn, 0)
+
+    unrolled(SAMPLES, turn)
 
     def move(s):
         table[pl.ds(slot_ref[s], 1), :] = rows[pl.ds(s, 1), :]
@@ -132,9 +140,11 @@
 
 def forward_kernel(
     groups, cap, cap_up, disp, params, arr, raw_out, wt, recv, msg, back, m0, tail_msg,
-    s1, r1, s2, r2,
+    master, master_sem, s1, r1, s2, r2,
 ):
     me = lax.axis_index("expert")
+    load = pltpu.make_async_copy(params, master, master_sem)
+    load.start()
     barrier = greet(groups, me)
     pl.semaphore_wait(barrier, groups - 1)
 
@@ -157,7 +167,8 @@
         return carry
 
     lax.fori_loop(1, groups, start, 0)
-    wt[...] = params[...].astype(BF16)
+    load.wait()
+    wt[...] = master[...].astype(BF16)
     pad_first(wt, m0)
     spot = lax.broadcasted_iota(jnp.int32, (4, LANES), 0) == lax.broadcasted_iota(
         jnp.int32, (4, LANES), 1
@@ -231,11 +242,10 @@
 
     move_rows(rows.shape[0], take)
 
-    def narrow(i, carry):
+    def narrow(i):
         eight[pl.ds(pl.multiple_of(8 * i, 8), 8), :] = rows[lane_block(i), :].T[0:8]
-        return carry
-
-    lax.fori_loop(0, SAMPLES, narrow, 0)
+
+    unrolled(SAMPLES, narrow)
     table[...] = jnp.zeros_like(table)
 
     table_rows = code_ref.shape[0]
@@ -316,12 +326,11 @@
     second_out[...] = new_second
     queries[...] = query_grad
 
-    def widen_back(i, carry):
+    def widen_back(i):
         piece = eight[pl.ds(pl.multiple_of(8 * i, 8), 8), :]
         rows[lane_block(i), :] = jnp.concatenate([piece, filler], axis=0).T
-        return carry
-
-    lax.fori_loop(0, SAMPLES, widen_back, 0)
+
+    unrolled(SAMPLES, widen_back)
 
     def put(s):
         table[pl.ds(slot_ref[s], 1), :] = rows[pl.ds(s, 1), :]
@@ -542,13 +551,15 @@
     table_scratch = pltpu.VMEM((slots_up + 8, LANES), F32)
     rows_scratch = pltpu.VMEM((sample_count, LANES), F32)
     msg_shape = (groups, 8, width)
+    local = (sample_count + slots_up) * LANES * 4 + 8 * 2**20
     disp = pl.pallas_call(
         functools.partial(place_kernel, groups, cap, cap_up),
         out_shape=shape((groups, cap, LANES), BF16),
         in_specs=[SMEM, VMEM],
         out_specs=VMEM,
         scratch_shapes=[rows_scratch, table_scratch],
-        compiler_params=pltpu.CompilerParams(vmem_limit_bytes=32 * 2**20),
+        compiler_params=pltpu.CompilerParams(vmem_limit_bytes=local),
+        cost_estimate=pl.CostEstimate(flops=0, bytes_accessed=6000 * sample_count, transcendentals=0),
         name="place",
     )(slot, features.transpose(1, 2, 0))
     sems = pltpu.SemaphoreType.DMA((groups,))
@@ -557,7 +568,7 @@
         out_shape=(
             shape((groups, cap, LANES), BF16), shape(msg_shape, F32), shape(params.shape, BF16),
         ),
-        in_specs=[VMEM] * 2,
+        in_specs=[VMEM, pl.BlockSpec(memory_space=pltpu.HBM)],
         out_specs=(VMEM,) * 3,
         scratch_shapes=[
             pltpu.VMEM((groups, cap, LANES), BF16),
@@ -565,11 +576,14 @@
             pltpu.VMEM(msg_shape, F32),
             pltpu.VMEM((2, LANES, NET_WIDTH), BF16),
             pltpu.VMEM((8, LANES), F32),
+            pltpu.VMEM(params.shape, F32),
+            pltpu.SemaphoreType.DMA,
             sems, sems, sems, sems,
         ],
         compiler_params=pltpu.CompilerParams(
             collective_id=0, has_side_effects=True, vmem_limit_bytes=32 * 2**20
         ),
+        cost_estimate=pl.CostEstimate(flops=0, bytes_accessed=16000 * sample_count, transcendentals=0),
         name="dispatch",
     )(disp, params)
     table_shape = shape(code_table.shape, F32)
@@ -588,7 +602,8 @@
             pltpu.VMEM((8 * groups, CODE_WIDTH), F32),
             pltpu.VMEM((8 * groups, LANES), F32),
         ],
-        compiler_params=pltpu.CompilerParams(vmem_limit_bytes=32 * 2**20),
+        compiler_params=pltpu.CompilerParams(vmem_limit_bytes=local),
+        cost_estimate=pl.CostEstimate(flops=0, bytes_accessed=12000 * sample_count, transcendentals=0),
         name="home",
     )(
         slot, raw_back, cell, spacing.T, ray_length[None, :], targets, local_image,
@@ -623,6 +638,7 @@
         compiler_params=pltpu.CompilerParams(
             collective_id=1, has_side_effects=True, vmem_limit_bytes=big
         ),
+        cost_estimate=pl.CostEstimate(flops=0, bytes_accessed=20000 * sample_count, transcendentals=0),
         name="backward",
     )(cot_msg, weights_bf, arr.reshape(all_rows, LANES))
     new_params, new_first, new_second = adam_update(params, param_grad, first_moment, second_moment)

time: 97 us -> 90 us (0.928)
  Pallas kernels: 89 us -> 82 us
    pallas_call x1, Pallas kernels: 18.3 us -> 13.8 us  [shards(): pl.pallas_call(functools.partial(home_kernel, groups, cap_up), out_shape=...]
    pallas_call x1, Pallas kernels: 8.25 us -> 5.4 us  [shards(): pl.pallas_call(functools.partial(place_kernel, groups, cap, cap_up), out_...]
where the time goes in v3:
time: 90 us; the launch traced here: 89.7 us
  Pallas kernels  82 us (91%)
  other arithmetic  4.38 us (5%)
  local copies, waits for them, and re-layouts  2.55 us (3%)
    pallas_call x1, Pallas kernels, shards(): pl.pallas_call(functools.partial(forward_kernel, groups, cap, cap_up), ou...  33.9 us
    pallas_call x1, Pallas kernels, shards(): pl.pallas_call(functools.partial(backward_kernel, groups, cap, cap_up), o...  28.9 us
    pallas_call x1, Pallas kernels, shards(): pl.pallas_call(functools.partial(home_kernel, groups, cap_up), out_shape=...  13.8 us
    pallas_call x1, Pallas kernels, shards(): pl.pallas_call(functools.partial(place_kernel, groups, cap, cap_up), out_...  5.4 us
    sub x1, other arithmetic, adam_update(): return (param_now - update, new_one, new_two)  2.98 us
    unnamed x24, local copies, waits for them, and re-layouts  2.55 us

profile of v3, /device:TPU:0, one launch (start us, length us, event | category | flops | bytes accessed | tf_op | source)
XLA Modules:
  0.0 89.7 jit_solution(9938297991563894870)
XLA Ops:
  0.6 0.7 subtract_bitcast_fusion.image_ref
  1.3 0.7 fusion.2.slot_ref
  2.0 0.0 copy-start.2
  2.0 1.0 %copy-done.2 = bf16[128,32,64]{0,2,1:T(8,128)(2,1)S(1)} copy-done((bf16[128,32,64]{0,2,1:T(8,128)(2,1)S(1)}, bf16[128,32,64]{0,2,1:T(8,128)(2,1)}, u32[]{:S(2)}) %copy-start.2) | copy-done | bytes 524312
  3.1 0.0 copy-start.3
  3.1 0.0 copy-start.4
  3.1 0.0 copy-start.5
  3.1 0.0 copy-start.6
  3.1 0.0 copy-start.7
  3.1 0.0 copy-start.8
  3.1 0.0 copy-start.9
  3.1 5.4 %place.1.disp = bf16[8,384,128]{2,1,0:T(8,128)(2,1)S(1)} custom-call(s32[4096]{0:T(1024)S(1)} %fusion.2.slot_ref, bf16[32,64,128]{2,1,0:T(8,128)(2,1)S(1)} %bitcast.21), custom_call_target="tpu_custom_call" | custom-call | bytes 24576000 | tf_op jit(solution)/shard_map/place/pallas_call | solution.py:555
  8.5 0.0 copy-start
  8.5 1.5 %copy-done = f32[2,848,256]{2,1,0:T(8,128)S(1)} copy-done((f32[2,848,256]{2,1,0:T(8,128)S(1)}, f32[2,848,256]{2,1,0:T(8,128)}, u32[]{:S(2)}) %copy-start) | copy-done | bytes 1736728
  10.0 0.0 copy-start.11
  10.0 33.9 %dispatch.1 = (bf16[8,384,128]{2,1,0:T(8,128)(2,1)S(1)}, f32[8,8,512]{2,1,0:T(8,128)S(1)}, bf16[2,848,256]{2,1,0:T(8,128)(2,1)S(1)}) custom-call(bf16[8,384,128]{2,1,0:T(8,128)(2,1)S(1)} %place.1.disp, f32[2,848,256]{2,1,0:T(8,128)S(1)} %copy-done), custom_call_target="tpu_custom_call" | custom-call | bytes 65536000 | tf_op jit(solution)/shard_map/dispatch/pallas_call | solution.py:566
  43.9 0.0 copy-done.3
  44.0 0.0 copy-done.4
  44.0 0.0 copy-done.5
  44.0 0.0 copy-done.6
  44.0 0.0 copy-done.7
  44.0 0.0 copy-done.8
  44.0 0.0 copy-done.9
  44.0 13.8 %home.1 = (f32[1,128]{1,0:T(1,128)}, f32[8,8,512]{2,1,0:T(8,128)S(1)}, f32[16,64]{1,0:T(8,128)}, f32[16,64]{1,0:T(8,128)}, f32[16,64]{1,0:T(8,128)}) custom-call(s32[4096]{0:T(1024)S(1)} %fusion.2.slot_ref, f32[8,8,512]{2,1,0:T(8,128)S(1)} %get-tuple-element.15.raw_ref, s32[32,128]{1,0:T(8,128)S(1)} %bitcast.22, f32[32,128]{1,0:T(8,128)S(1)} %bitcast.23, ...), custom_call_target="tpu_custom_call" | custom-call | bytes 49152000 | tf_op jit(solution)/shard_map/home/pallas_call | solution.py:590
  57.8 0.0 copy-start.1
  57.8 0.0 copy-start.10
  57.8 28.9 %backward.1 = f32[2,848,256]{2,1,0:T(8,128)S(1)} custom-call(f32[8,8,512]{2,1,0:T(8,128)S(1)} %get-tuple-element.17.msg, bf16[2,848,256]{2,1,0:T(8,128)(2,1)S(1)} %get-tuple-element.18.wt, bf16[3072,128]{1,0:T(8,128)(2,1)S(1)} %bitcast.20), custom_call_target="tpu_custom_call" | custom-call | bytes 81920000 | tf_op jit(solution)/shard_map/backward/pallas_call | solution.py:614
  86.7 0.0 copy-done.11
  86.7 0.0 copy-done.1
  86.7 0.0 copy-done.10
  86.7 3.0 %divide_subtract_fusion = (f32[2,848,256]{2,1,0:T(8,128)}, f32[2,848,256]{2,1,0:T(8,128)}, f32[2,848,256]{2,1,0:T(8,128)}) fusion(f32[2,848,256]{2,1,0:T(8,128)S(1)} %copy-done.1, f32[2,848,256]{2,1,0:T(8,128)S(1)} %backward.1, f32[2,848,256]{2,1,0:T(8,128)S(1)} %copy-done.10, f32[2,848,256]{2,1,0:T(8,128)S(1)} %copy-done.11), kind=kLoop, calls=%fused_computation.2 | loop fusion | flops 5210112 | bytes 12156928 | tf_op jit(solution)/shard_map/sub | solution.py:47
Async XLA Ops:
  2.0 1.0 %copy-start.2 = (bf16[128,32,64]{0,2,1:T(8,128)(2,1)S(1)}, bf16[128,32,64]{0,2,1:T(8,128)(2,1)}, u32[]{:S(2)}) copy-start(bf16[128,32,64]{0,2,1:T(8,128)(2,1)} %param.13) | copy-start | bytes 1572868
  3.1 40.9 %copy-start.3 = (s32[128,32]{0,1:T(8,128)S(1)}, s32[128,32]{0,1:T(8,128)}, u32[]{:S(2)}) copy-start(s32[128,32]{0,1:T(8,128)} %param.17) | copy-start | bytes 49156
  3.1 40.9 %copy-start.4 = (f32[128,32]{0,1:T(8,128)S(1)}, f32[128,32]{0,1:T(8,128)}, u32[]{:S(2)}) copy-start(f32[128,32]{0,1:T(8,128)} %param.14) | copy-start | bytes 49156
  3.1 40.9 %copy-start.5 = (f32[16,64]{1,0:T(8,128)S(1)}, f32[16,64]{1,0:T(8,128)}, u32[]{:S(2)}) copy-start(f32[16,64]{1,0:T(8,128)} %code_ref.1) | copy-start | bytes 12292
  3.1 40.9 %copy-start.6 = (f32[16,64]{1,0:T(8,128)S(1)}, f32[16,64]{1,0:T(8,128)}, u32[]{:S(2)}) copy-start(f32[16,64]{1,0:T(8,128)} %first_ref.1) | copy-start | bytes 12292
  3.1 40.9 %copy-start.7 = (f32[16,64]{1,0:T(8,128)S(1)}, f32[16,64]{1,0:T(8,128)}, u32[]{:S(2)}) copy-start(f32[16,64]{1,0:T(8,128)} %second_ref.1) | copy-start | bytes 12292
  3.1 40.9 %copy-start.8 = (f32[3,128]{1,0:T(4,128)S(1)}, f32[3,128]{1,0:T(4,128)}, u32[]{:S(2)}) copy-start(f32[3,128]{1,0:T(4,128)} %target_ref.1) | copy-start | bytes 4612
  3.1 40.9 %copy-start.9 = (s32[128]{0:T(128)S(1)}, s32[128]{0:T(128)}, u32[]{:S(2)}) copy-start(s32[128]{0:T(128)} %param.16) | copy-start | bytes 1540
  8.5 1.5 %copy-start = (f32[2,848,256]{2,1,0:T(8,128)S(1)}, f32[2,848,256]{2,1,0:T(8,128)}, u32[]{:S(2)}) copy-start(f32[2,848,256]{2,1,0:T(8,128)} %params.1) | copy-start | bytes 5210116
  10.0 76.7 %copy-start.11 = (f32[2,848,256]{2,1,0:T(8,128)S(1)}, f32[2,848,256]{2,1,0:T(8,128)}, u32[]{:S(2)}) copy-start(f32[2,848,256]{2,1,0:T(8,128)} %param.22) | copy-start | bytes 5210116
  57.8 28.9 %copy-start.1 = (f32[2,848,256]{2,1,0:T(8,128)S(1)}, f32[2,848,256]{2,1,0:T(8,128)}, u32[]{:S(2)}) copy-start(f32[2,848,256]{2,1,0:T(8,128)} %params.1) | copy-start | bytes 5210116
  57.8 28.9 %copy-start.10 = (f32[2,848,256]{2,1,0:T(8,128)S(1)}, f32[2,848,256]{2,1,0:T(8,128)}, u32[]{:S(2)}) copy-start(f32[2,848,256]{2,1,0:T(8,128)} %param.21) | copy-start | bytes 5210116
